TPU v7x, 32 devices: a whole 2x2x4 slice. The times are simulated.
32 devices in a mesh: groups: 2 (over x), tensor: 8 (over z, y), batch: 2 (over core).
Axes of the slice: x: 2, y: 2, z: 4, core: 2. Of those that a mesh axis runs over, the one named last changes fastest.
Arguments:
- hidden: bfloat16 [256, 2, 8192], P(('groups', 'tensor', 'batch')), parts along dimension 0, may hold values from -6 to 6
- wq: bfloat16 [8192, 8192], P(None, 'tensor'), may hold values from -0.0625 to 0.0625
- wkv: bfloat16 [8192, 2048], P(None, 'tensor'), may hold values from -0.0625 to 0.0625
- cache_pool: bfloat16 [512, 128, 2048], P(('groups', 'tensor', 'batch')), parts along dimension 0, may hold values from -240 to 240
- page_table: int32 [256, 2], P(('groups', 'tensor', 'batch')), parts along dimension 0, may hold values from 0 to 15, as said below
- ctx_len: int32 [256], P(('groups', 'tensor', 'batch')), parts along dimension 0, may hold values from 1 to 256
- prompt_slot: int32 [32], P(('groups', 'tensor', 'batch')), parts along dimension 0, may hold values from 0 to 7
- prompt_kv: bfloat16 [32, 128, 2048], P(('groups', 'batch'), None, 'tensor'), parts along dimension 0, may hold values from -6 to 6
Outputs:
- attended: bfloat16 [256, 2, 8192], P(('groups', 'tensor', 'batch')), parts along dimension 0
There are 2 independent parts, one for each index of `groups`. A program takes and returns all parts, laid end to end along the dimension named above; an argument that names none is the same for every part. Nothing has to cross between parts.
Inputs may be any that keep to these rules, and one draw needn't show every extreme that they name: `page_table`: within each block of 8 sequences the entries name each of that block's 16 local pages exactly once; entry p holds the sequence's tokens p * 128 to (p + 1) * 128 - 1.
All inputs are finite; a program needn't handle non-finite values.
Results may differ from a plain program's by a relative error of at most 0.012.
Values may be sent and summed in bfloat16 or wider, within the bound.
No kernel may reach another device: no remote copies, remote signals or barrier semaphores. Data moves between devices by JAX's collectives and lax.ppermute only.
A program may use at most 128 MiB of HBM per device.

v0:
```python
import functools

import jax
import jax.numpy as jnp
from jax import lax
from jax.experimental import pallas as pl
from jax.experimental.pallas import tpu as pltpu
from jax.sharding import PartitionSpec as P


QUERY_HEADS = 64
KEY_VALUE_HEADS = 8
HEAD_SIZE = 128
GROUP = QUERY_HEADS // KEY_VALUE_HEADS
STEPS = 2
MASKED = -1e30
PROJECT_LIMIT = 48 << 20
ATTEND_LIMIT = 52 << 20


def attend_kernel(
    table_ref, lens_ref, slot_ref, q_ref, kv_ref, prompt_ref, pool_ref, out_ref,
    pages, q_all, acc, top_all, sum_all, q_f32, sems, *, seqs, q_width, kv_off, kv_width, prompt_width,
):
    span_pages = table_ref.shape[0] // seqs
    page_rows = pool_ref.shape[1]
    span = span_pages * page_rows
    rows = STEPS * GROUP
    all_rows = KEY_VALUE_HEADS * rows
    value_at = KEY_VALUE_HEADS * HEAD_SIZE

    def page_copy(s, p):
        return pltpu.make_async_copy(
            pool_ref.at[table_ref[s * span_pages + p]],
            pages.at[s, pl.ds(p * page_rows, page_rows)],
            sems.at[s, p],
        )

    for s in range(seqs):
        for p in range(span_pages):
            page_copy(s, p).start()

    for h in range(QUERY_HEADS):
        k, g = h // GROUP, h % GROUP
        block, at = (h * HEAD_SIZE) // q_width, (h * HEAD_SIZE) % q_width
        q_f32[k, pl.ds(g, seqs * STEPS, stride=GROUP), :] = q_ref[block, :, at : at + HEAD_SIZE].astype(jnp.float32)
    q_all[...] = q_f32[...].astype(jnp.bfloat16)

    def new_tile(col):
        block, at = col // kv_width, kv_off + col % kv_width
        return kv_ref[block, :, at : at + HEAD_SIZE]

    def prompt_tile(col):
        block, at = col // prompt_width, col % prompt_width
        return prompt_ref[block, :, at : at + HEAD_SIZE]

    def scaled(q, keys):
        return lax.dot_general(
            q, keys, (((1,), (1,)), ((), ())), preferred_element_type=jnp.float32
        ) * HEAD_SIZE ** (-0.5)

    def mix(w, values):
        return jnp.dot(w.astype(jnp.bfloat16), values, preferred_element_type=jnp.float32)

    where_key = lax.broadcasted_iota(jnp.int32, (all_rows, span), 1)
    step_of = (lax.broadcasted_iota(jnp.int32, (all_rows, seqs * STEPS), 0) // GROUP) % STEPS
    new_at = lax.broadcasted_iota(jnp.int32, (all_rows, seqs * STEPS), 1)

    def one_sequence(s, carry):
        for p in range(span_pages):
            page_copy(s, p).wait()

        def cached(col):
            return pages[s, :, col : col + HEAD_SIZE]

        at = pl.multiple_of(s * rows, rows)
        q_s = [q_all[k, pl.ds(at, rows), :] for k in range(KEY_VALUE_HEADS)]
        sc = jnp.concatenate(
            [scaled(q_s[k], cached(k * HEAD_SIZE)) for k in range(KEY_VALUE_HEADS)]
        )
        sn = jnp.concatenate([scaled(q_s[k], new_tile(k * HEAD_SIZE)) for k in range(KEY_VALUE_HEADS)])
        sc = jnp.where(where_key < lens_ref[s], sc, MASKED)
        offset = new_at - s * STEPS
        sn = jnp.where((offset >= 0) & (offset <= step_of), sn, MASKED)
        top = jnp.maximum(jnp.max(sc, axis=1, keepdims=True), jnp.max(sn, axis=1, keepdims=True))
        ec = jnp.exp(sc - top)
        en = jnp.exp(sn - top)
        total = jnp.sum(ec, axis=1, keepdims=True) + jnp.sum(en, axis=1, keepdims=True)
        for k in range(KEY_VALUE_HEADS):
            part = slice(k * rows, (k + 1) * rows)
            col = value_at + k * HEAD_SIZE
            acc[k, pl.ds(at, rows), :] = mix(ec[part], cached(col)) + mix(
                en[part], new_tile(col)
            )
            top_all[k, pl.ds(at, rows), :] = jnp.broadcast_to(top[part], (rows, HEAD_SIZE))
            sum_all[k, pl.ds(at, rows), :] = jnp.broadcast_to(total[part], (rows, HEAD_SIZE))
        return carry

    lax.fori_loop(0, seqs, one_sequence, 0, unroll=False)

    at = pl.multiple_of(slot_ref[0] * rows, rows)
    for k in range(KEY_VALUE_HEADS):
        mine = (k, pl.ds(at, rows), slice(None))
        sp = scaled(q_all[mine], prompt_tile(k * HEAD_SIZE))
        before = top_all[mine]
        top = jnp.maximum(before, jnp.max(sp, axis=1, keepdims=True))
        ep = jnp.exp(sp - top[:, :1])
        keep = jnp.exp(before - top)
        sum_all[mine] = sum_all[mine] * keep + jnp.sum(ep, axis=1, keepdims=True)
        acc[mine] = acc[mine] * keep + mix(ep, prompt_tile(value_at + k * HEAD_SIZE))

    acc[...] = acc[...] / sum_all[...]
    for h in range(QUERY_HEADS):
        k, g = h // GROUP, h % GROUP
        out_ref[:, h * HEAD_SIZE : (h + 1) * HEAD_SIZE] = acc[
            k, pl.ds(g, seqs * STEPS, stride=GROUP), :
        ].astype(jnp.bfloat16)


def attend(joined, q_width, prompt, pool, table, lens, slot):
    blocks, tokens, width = joined.shape
    seqs = tokens // STEPS
    kv_width = width - q_width
    kv_off = q_width
    kv = joined
    if kv_width % HEAD_SIZE:
        kv = joined[:, :, q_width:].transpose(1, 0, 2).reshape(1, tokens, blocks * kv_width)
        prompt = prompt.transpose(1, 0, 2).reshape(1, prompt.shape[1], blocks * kv_width)
        kv_width, kv_off = blocks * kv_width, 0
    rows = seqs * STEPS * GROUP
    smem = pl.BlockSpec(memory_space=pltpu.SMEM)
    vmem = pl.BlockSpec(memory_space=pltpu.VMEM)
    kernel = functools.partial(
        attend_kernel, seqs=seqs, q_width=q_width, kv_off=kv_off, kv_width=kv_width, prompt_width=prompt.shape[2]
    )
    big = pltpu.VMEM((KEY_VALUE_HEADS, rows, HEAD_SIZE), jnp.float32)
    return pl.pallas_call(
        kernel,
        out_shape=jax.ShapeDtypeStruct((tokens, QUERY_HEADS * HEAD_SIZE), jnp.bfloat16),
        in_specs=[smem, smem, smem, vmem, vmem, vmem, pl.BlockSpec(memory_space=pl.ANY)],
        out_specs=vmem,
        scratch_shapes=[
            pltpu.VMEM((seqs, table.shape[1] * pool.shape[1], pool.shape[2]), jnp.bfloat16),
            pltpu.VMEM((KEY_VALUE_HEADS, rows, HEAD_SIZE), jnp.bfloat16),
            big, big, big, big,
            pltpu.SemaphoreType.DMA((seqs, table.shape[1])),
        ],
        compiler_params=pltpu.CompilerParams(vmem_limit_bytes=ATTEND_LIMIT),
        name="attend",
    )(table.reshape(-1), lens, slot, joined, kv, prompt, pool)


def gather_blocks(own, axis, size):
    me = lax.axis_index(axis)
    line = size // 2
    place, side = me // 2, me % 2

    def hop(x, step, first, last):
        return lax.ppermute(
            x, axis, [(2 * c + p, 2 * (c + step) + p) for c in range(first, last + 1) for p in (0, 1)]
        )

    def swap(x, first, last):
        return lax.ppermute(x, axis, [(2 * c + p, 2 * c + 1 - p) for c in range(first, last + 1) for p in (0, 1)])

    up, down = {0: own}, {0: own}
    up_pair, down_pair = {}, {}
    near = swap(own, 0, line - 1)
    found = [((own,), 0, me), ((near,), 0, 2 * place + 1 - side)]
    for s in range(1, line):
        up[s] = hop(up[s - 1], 1, s - 1, line - 2)
        down[s] = hop(down[s - 1], -1, 1, line - s)
        up_pair[s] = swap(up[s], s, line - 1)
        down_pair[s] = swap(down[s], 0, line - 1 - s)
    for s in range(1, line):
        other = (place + line - s) % line
        first = place >= s
        found.append(((up[s], down[line - s]), 1 - first.astype(jnp.int32), 2 * other + side))
        found.append(((up_pair[s], down_pair[line - s]), 1 - first.astype(jnp.int32), 2 * other + 1 - side))
    return found, (up[line - 1], down[line - 1])


def project_kernel(owner_ref, choice_ref, *refs, tiles, counts):
    blocks = sum(counts)
    sources = refs[:blocks]
    wq_ref, wkv_ref, out_ref, x_here, w_here, x_sems, w_sems = refs[blocks:]
    size, tokens, _ = out_ref.shape
    q_width = wq_ref.shape[1]

    def fetch(j, source):
        rows = pl.ds(pl.multiple_of(owner_ref[j] * tokens, tokens), tokens)
        return pltpu.make_async_copy(source, x_here.at[rows], x_sems.at[j])

    at = 0
    firsts = []
    for j, count in enumerate(counts):
        firsts.append(sources[at])
        if count == 1:
            fetch(j, sources[at]).start()
        else:
            one, other = sources[at], sources[at + 1]

            @pl.when(choice_ref[j] == 0)
            def _():
                fetch(j, one).start()

            @pl.when(choice_ref[j] != 0)
            def _():
                fetch(j, other).start()

        at += count
    copies = []
    for i, (at, width) in enumerate(tiles):
        source = wq_ref.at[:, pl.ds(at, width)] if at < q_width else wkv_ref.at[:, pl.ds(at - q_width, width)]
        copies.append(pltpu.make_async_copy(source, w_here.at[:, pl.ds(at, width)], w_sems.at[i]))
    for c in copies:
        c.start()
    for j, source in enumerate(firsts):
        fetch(j, source).wait()

    for c, (at, width) in zip(copies, tiles):
        c.wait()
        cols = slice(at, at + width)
        y = jnp.dot(x_here[...], w_here[:, cols], preferred_element_type=jnp.float32).astype(jnp.bfloat16)
        for j in range(size):
            out_ref[j, :, cols] = y[j * tokens : (j + 1) * tokens]


def project(found, wq, wkv):
    size = len(found)
    tokens = found[0][0][0].shape[0]
    depth, q_width = wq.shape
    width = q_width + wkv.shape[1]
    wide = 2 * HEAD_SIZE
    tiles = [(at, min(wide, q_width - at)) for at in range(0, q_width, wide)]
    tiles += [(at, min(HEAD_SIZE, width - at)) for at in range(q_width, width, HEAD_SIZE)]
    counts = [len(options) for options, _, _ in found]
    sources = [block for options, _, _ in found for block in options]
    choices = jnp.stack([jnp.asarray(choice, jnp.int32) for _, choice, _ in found])
    owners = jnp.stack([jnp.asarray(owner, jnp.int32) for _, _, owner in found])
    smem = pl.BlockSpec(memory_space=pltpu.SMEM)
    vmem = pl.BlockSpec(memory_space=pltpu.VMEM)
    hbm = pl.BlockSpec(memory_space=pl.ANY)
    return pl.pallas_call(
        functools.partial(project_kernel, tiles=tiles, counts=counts),
        out_shape=jax.ShapeDtypeStruct((size, tokens, width), jnp.bfloat16),
        in_specs=[smem, smem] + [hbm] * len(sources) + [hbm, hbm],
        out_specs=vmem,
        scratch_shapes=[
            pltpu.VMEM((size * tokens, depth), wq.dtype),
            pltpu.VMEM((depth, width), wq.dtype),
            pltpu.SemaphoreType.DMA((size,)),
            pltpu.SemaphoreType.DMA((len(tiles),)),
        ],
        compiler_params=pltpu.CompilerParams(vmem_limit_bytes=PROJECT_LIMIT),
        cost_estimate=pl.CostEstimate(
            flops=2 * size * tokens * depth * width,
            bytes_accessed=2 * depth * (size * tokens + width),
            transcendentals=0,
        ),
        name="project",
    )(owners, choices, *sources, wq, wkv)


def per_device(size, hidden, wq, wkv, cache_pool, page_table, ctx_len, prompt_slot, prompt_kv):
    tokens = hidden.shape[0] * hidden.shape[1]
    own = hidden.reshape(tokens, hidden.shape[2])
    found, late = gather_blocks(own, "tensor", size)
    prompt_kv, _ = lax.optimization_barrier((prompt_kv, late))
    prompt = lax.all_to_all(prompt_kv, "tensor", split_axis=0, concat_axis=0, tiled=True)
    joined = project(found, wq, wkv)
    joined, prompt = lax.optimization_barrier((joined, prompt))
    back = lax.all_to_all(joined, "tensor", split_axis=0, concat_axis=0, tiled=True)
    out = attend(back, wq.shape[1], prompt, cache_pool, page_table, ctx_len, prompt_slot)
    return out.reshape(hidden.shape[0], hidden.shape[1], -1)


def solution(mesh):
    placed = (
        P(("groups", "tensor", "batch"), None, None),
        P(None, "tensor"),
        P(None, "tensor"),
        P(("groups", "tensor", "batch"), None, None),
        P(("groups", "tensor", "batch"), None),
        P(("groups", "tensor", "batch")),
        P(("groups", "tensor", "batch")),
        P(("groups", "batch"), None, "tensor"),
    )
    return jax.shard_map(
        functools.partial(per_device, mesh.shape["tensor"]),
        mesh=mesh,
        in_specs=placed,
        out_specs=P(("groups", "tensor", "batch"), None, None),
        check_vma=False,
    )
```

profile of v0, /device:TPU:0, one launch (start us, length us, event | category | flops | bytes accessed | tf_op | source)
XLA Modules:
  0.0 97.6 jit_solution(15430379945490599840)
XLA Ops:
  0.0 1.0 %reshape.10.refs_0_ = bf16[16,8192]{1,0:T(8,128)(2,1)S(1)} reshape(bf16[8,2,8192]{2,1,0:T(2,128)(2,1)} %param.8) | data formatting | bytes 524288 | tf_op jit(solution)/shard_map/reshape | solution.py:267
  1.1 5.0 %collective-permute-start.1 = (bf16[16,8192]{1,0:T(8,128)(2,1)S(1)}, bf16[16,8192]{1,0:T(8,128)(2,1)S(1)}, u32[]{:S(2)}, u32[]{:S(2)}) collective-permute-start(bf16[16,8192]{1,0:T(8,128)(2,1)S(1)} %reshape.10.refs_0_), channel_id=1, source_target_pairs={{0,4},{2,6},{4,8},{6,10},{8,12},{10,14},{1,5},{3,7},{5,9},{7,11},{... | collective-permute-start | bytes 786440 | tf_op jit(solution)/shard_map/ppermute | solution.py:159
  6.0 1.3 %collective-permute-start.2 = (bf16[16,8192]{1,0:T(8,128)(2,1)S(1)}, bf16[16,8192]{1,0:T(8,128)(2,1)S(1)}, u32[]{:S(2)}, u32[]{:S(2)}) collective-permute-start(bf16[16,8192]{1,0:T(8,128)(2,1)S(1)} %reshape.10.refs_0_), channel_id=1, source_target_pairs={{4,0},{6,2},{8,4},{10,6},{12,8},{14,10},{5,1},{7,3},{9,5},{11,7},{... | collective-permute-start | bytes 786440 | tf_op jit(solution)/shard_map/ppermute | solution.py:159
  7.3 4.2 %collective-permute-done.1.refs_2_ = bf16[16,8192]{1,0:T(8,128)(2,1)S(1)} collective-permute-done((bf16[16,8192]{1,0:T(8,128)(2,1)S(1)}, bf16[16,8192]{1,0:T(8,128)(2,1)S(1)}, u32[]{:S(2)}, u32[]{:S(2)}) %collective-permute-start.1) | collective-permute-done | bytes 262176 | tf_op jit(solution)/shard_map/ppermute | solution.py:159
  11.6 0.7 collective-permute-start.7
  12.2 3.5 %collective-permute-done.2.refs_11_ = bf16[16,8192]{1,0:T(8,128)(2,1)S(1)} collective-permute-done((bf16[16,8192]{1,0:T(8,128)(2,1)S(1)}, bf16[16,8192]{1,0:T(8,128)(2,1)S(1)}, u32[]{:S(2)}, u32[]{:S(2)}) %collective-permute-start.2) | collective-permute-done | bytes 262176 | tf_op jit(solution)/shard_map/ppermute | solution.py:159
  15.7 1.3 %collective-permute-start.3 = (bf16[16,8192]{1,0:T(8,128)(2,1)S(1)}, bf16[16,8192]{1,0:T(8,128)(2,1)S(1)}, u32[]{:S(2)}, u32[]{:S(2)}) collective-permute-start(bf16[16,8192]{1,0:T(8,128)(2,1)S(1)} %collective-permute-done.2.refs_11_), channel_id=1, source_target_pairs={{4,0},{6,2},{8,4},{10,6},{5,1},{7,3},{9,5},{11,7},{20,16},{22,18},... | collective-permute-start | bytes 786440 | tf_op jit(solution)/shard_map/ppermute | solution.py:159
  17.0 0.0 collective-permute-done.7.refs_6_
  17.0 0.7 collective-permute-start.10
  17.7 6.9 %collective-permute-done.3.refs_7_ = bf16[16,8192]{1,0:T(8,128)(2,1)S(1)} collective-permute-done((bf16[16,8192]{1,0:T(8,128)(2,1)S(1)}, bf16[16,8192]{1,0:T(8,128)(2,1)S(1)}, u32[]{:S(2)}, u32[]{:S(2)}) %collective-permute-start.3) | collective-permute-done | bytes 262176 | tf_op jit(solution)/shard_map/ppermute | solution.py:159
  24.6 1.3 %collective-permute-start.4 = (bf16[16,8192]{1,0:T(8,128)(2,1)S(1)}, bf16[16,8192]{1,0:T(8,128)(2,1)S(1)}, u32[]{:S(2)}, u32[]{:S(2)}) collective-permute-start(bf16[16,8192]{1,0:T(8,128)(2,1)S(1)} %collective-permute-done.3.refs_7_), channel_id=1, source_target_pairs={{4,0},{6,2},{5,1},{7,3},{20,16},{22,18},{21,17},{23,19}} | collective-permute-start | bytes 786440 | tf_op jit(solution)/shard_map/ppermute | solution.py:159
  25.9 0.0 collective-permute-done.10.refs_10_
  25.9 7.0 %collective-permute-done.4.refs_3_ = bf16[16,8192]{1,0:T(8,128)(2,1)S(1)} collective-permute-done((bf16[16,8192]{1,0:T(8,128)(2,1)S(1)}, bf16[16,8192]{1,0:T(8,128)(2,1)S(1)}, u32[]{:S(2)}, u32[]{:S(2)}) %collective-permute-start.4) | collective-permute-done | bytes 262176 | tf_op jit(solution)/shard_map/ppermute | solution.py:159
  32.9 3.5 %all-to-all-start = ((bf16[8,128,256]{2,1,0:T(8,128)(2,1)}), bf16[8,128,256]{2,1,0:T(8,128)(2,1)S(1)}, u32[]{:S(2)}, u32[]{:S(2)}) async-start(bf16[8,128,256]{2,1,0:T(8,128)(2,1)} %param.15), calls=%async_computation | async-start | bytes 1048576 | tf_op jit(solution)/shard_map/all_to_all | solution.py:270
  36.4 1.9 %collective-permute-start = (bf16[16,8192]{1,0:T(8,128)(2,1)S(1)}, bf16[16,8192]{1,0:T(8,128)(2,1)S(1)}, u32[]{:S(2)}, u32[]{:S(2)}) collective-permute-start(bf16[16,8192]{1,0:T(8,128)(2,1)S(1)} %reshape.10.refs_0_), channel_id=1, source_target_pairs={{0,2},{2,0},{4,6},{6,4},{8,10},{10,8},{12,14},{14,12},{1,3},{3,1},... | collective-permute-start | bytes 786440 | tf_op jit(solution)/shard_map/ppermute | solution.py:164
  38.3 2.1 %collective-permute-start.12 = (bf16[16,8192]{1,0:T(8,128)(2,1)S(1)}, bf16[16,8192]{1,0:T(8,128)(2,1)S(1)}, u32[]{:S(2)}, u32[]{:S(2)}) collective-permute-start(bf16[16,8192]{1,0:T(8,128)(2,1)S(1)} %collective-permute-done.2.refs_11_), channel_id=1, source_target_pairs={{0,2},{2,0},{4,6},{6,4},{8,10},{10,8},{1,3},{3,1},{5,7},{7,5},{9,1... | collective-permute-start | bytes 786440 | tf_op jit(solution)/shard_map/ppermute | solution.py:164
  40.4 0.7 collective-permute-start.5
  41.1 0.7 collective-permute-start.8
  41.7 3.8 %collective-permute-start.9 = (bf16[16,8192]{1,0:T(8,128)(2,1)S(1)}, bf16[16,8192]{1,0:T(8,128)(2,1)}, u32[]{:S(2)}, u32[]{:S(2)}) collective-permute-start(bf16[16,8192]{1,0:T(8,128)(2,1)S(1)} %collective-permute-done.3.refs_7_), channel_id=1, source_target_pairs={{0,2},{2,0},{4,6},{6,4},{1,3},{3,1},{5,7},{7,5},{16,18},{18,16},{2... | collective-permute-start | bytes 786440 | tf_op jit(solution)/shard_map/ppermute | solution.py:164
  45.5 4.4 %collective-permute-done.refs_1_ = bf16[16,8192]{1,0:T(8,128)(2,1)S(1)} collective-permute-done((bf16[16,8192]{1,0:T(8,128)(2,1)S(1)}, bf16[16,8192]{1,0:T(8,128)(2,1)S(1)}, u32[]{:S(2)}, u32[]{:S(2)}) %collective-permute-start) | collective-permute-done | bytes 262176 | tf_op jit(solution)/shard_map/ppermute | solution.py:164
  49.9 1.4 %collective-permute-start.11 = (bf16[16,8192]{1,0:T(8,128)(2,1)S(1)}, bf16[16,8192]{1,0:T(8,128)(2,1)}, u32[]{:S(2)}, u32[]{:S(2)}) collective-permute-start(bf16[16,8192]{1,0:T(8,128)(2,1)S(1)} %collective-permute-done.10.refs_10_), channel_id=1, source_target_pairs={{12,14},{14,12},{13,15},{15,13},{28,30},{30,28},{29,31},{31,29}} | collective-permute-start | bytes 786440 | tf_op jit(solution)/shard_map/ppermute | solution.py:164
  51.2 4.3 %collective-permute-done.12.refs_13_ = bf16[16,8192]{1,0:T(8,128)(2,1)S(1)} collective-permute-done((bf16[16,8192]{1,0:T(8,128)(2,1)S(1)}, bf16[16,8192]{1,0:T(8,128)(2,1)S(1)}, u32[]{:S(2)}, u32[]{:S(2)}) %collective-permute-start.12) | collective-permute-done | bytes 262176 | tf_op jit(solution)/shard_map/ppermute | solution.py:164
  55.5 2.3 %collective-permute-start.6 = (bf16[16,8192]{1,0:T(8,128)(2,1)S(1)}, bf16[16,8192]{1,0:T(8,128)(2,1)}, u32[]{:S(2)}, u32[]{:S(2)}) collective-permute-start(bf16[16,8192]{1,0:T(8,128)(2,1)S(1)} %collective-permute-done.4.refs_3_), channel_id=1, source_target_pairs={{0,2},{2,0},{1,3},{3,1},{16,18},{18,16},{17,19},{19,17}} | collective-permute-start | bytes 786440 | tf_op jit(solution)/shard_map/ppermute | solution.py:164
  57.9 0.1 stack.54.choice_ref
  58.0 0.1 stack.50.owner_ref
  58.1 0.0 copy-start.1
  58.1 0.0 copy-start
  58.1 0.0 collective-permute-done.5.refs_4_
  58.1 0.0 collective-permute-done.8.refs_8_
  58.1 3.1 %collective-permute-done.9.refs_9_ = bf16[16,8192]{1,0:T(8,128)(2,1)} collective-permute-done((bf16[16,8192]{1,0:T(8,128)(2,1)S(1)}, bf16[16,8192]{1,0:T(8,128)(2,1)}, u32[]{:S(2)}, u32[]{:S(2)}) %collective-permute-start.9) | collective-permute-done | bytes 262176 | tf_op jit(solution)/shard_map/ppermute | solution.py:164
  61.2 0.0 collective-permute-done.11.refs_12_
  61.2 2.9 %collective-permute-done.6.refs_5_ = bf16[16,8192]{1,0:T(8,128)(2,1)} collective-permute-done((bf16[16,8192]{1,0:T(8,128)(2,1)S(1)}, bf16[16,8192]{1,0:T(8,128)(2,1)}, u32[]{:S(2)}, u32[]{:S(2)}) %collective-permute-start.6) | collective-permute-done | bytes 262176 | tf_op jit(solution)/shard_map/ppermute | solution.py:164
  64.1 10.2 %project.1 = bf16[8,16,1280]{2,1,0:T(8,128)(2,1)} custom-call(s32[8]{0:T(128)S(1)} %stack.50.owner_ref, s32[8]{0:T(128)S(1)} %stack.54.choice_ref, bf16[16,8192]{1,0:T(8,128)(2,1)S(1)} %reshape.10.refs_0_, bf16[16,8192]{1,0:T(8,128)(2,1)S(1)} %collective-permute-done.refs_1_, bf16[16,8192]{1,0:T(8,128)(2,1)S(1)} %collective-permute-done.1.refs_2_, ...), custom_call_target="tpu_custom_call" | custom-call | flops 2684354560 | bytes 23068672 | tf_op jit(solution)/shard_map/project/pallas_call | solution.py:244
  74.3 0.0 all-to-all-done.prompt_ref
  74.4 4.6 %all-to-all-start.1 = ((bf16[8,16,1280]{2,1,0:T(8,128)(2,1)}), bf16[8,16,1280]{2,1,0:T(8,128)(2,1)S(1)}, u32[]{:S(2)}, u32[]{:S(2)}) async-start(bf16[8,16,1280]{2,1,0:T(8,128)(2,1)} %project.1), calls=%async_computation.1 | async-start | bytes 655360 | tf_op jit(solution)/shard_map/all_to_all | solution.py:273
  79.0 0.0 copy-done.1
  79.0 0.1 copy.10
  79.1 0.1 reshape.9.table_ref
  79.8 7.8 %all-to-all-done.1.q_ref.kv_ref = bf16[8,16,1280]{2,1,0:T(8,128)(2,1)S(1)} async-done(((bf16[8,16,1280]{2,1,0:T(8,128)(2,1)}), bf16[8,16,1280]{2,1,0:T(8,128)(2,1)S(1)}, u32[]{:S(2)}, u32[]{:S(2)}) %all-to-all-start.1) | async-done | bytes 327712 | tf_op jit(solution)/shard_map/all_to_all | solution.py:273
  87.6 0.0 copy-done
  87.6 9.1 %attend.1 = bf16[16,8192]{1,0:T(8,128)(2,1)S(1)} custom-call(s32[16]{0:T(128)S(1)} %reshape.9.table_ref, s32[8]{0:T(128)S(1)} %copy-done, s32[1]{0:T(128)S(6)} %copy.11.slot_ref, bf16[8,16,1280]{2,1,0:T(8,128)(2,1)S(1)} %all-to-all-done.1.q_ref.kv_ref, bf16[8,16,1280]{2,1,0:T(8,128)(2,1)S(1)} %all-to-all-done.1.q_ref.kv_ref, ...), custom_call_target="tpu_custom_call" | custom-call | tf_op jit(solution)/shard_map/attend/pallas_call | solution.py:137
  96.7 0.9 reshape.11
  (1 shorter events, 0.0 us)
Async XLA Ops:
  1.1 10.5 %collective-permute-start.1 = (bf16[16,8192]{1,0:T(8,128)(2,1)S(1)}, bf16[16,8192]{1,0:T(8,128)(2,1)S(1)}, u32[]{:S(2)}, u32[]{:S(2)}) collective-permute-start(bf16[16,8192]{1,0:T(8,128)(2,1)S(1)} %reshape.10.refs_0_), channel_id=1, source_target_pairs={{0,4},{2,6},{4,8},{6,10},{8,12},{10,14},{1,5},{3,7},{5,9},{7,11},{... | collective-permute-start | bytes 786440 | tf_op jit(solution)/shard_map/ppermute | solution.py:159
  6.0 9.7 %collective-permute-start.2 = (bf16[16,8192]{1,0:T(8,128)(2,1)S(1)}, bf16[16,8192]{1,0:T(8,128)(2,1)S(1)}, u32[]{:S(2)}, u32[]{:S(2)}) collective-permute-start(bf16[16,8192]{1,0:T(8,128)(2,1)S(1)} %reshape.10.refs_0_), channel_id=1, source_target_pairs={{4,0},{6,2},{8,4},{10,6},{12,8},{14,10},{5,1},{7,3},{9,5},{11,7},{... | collective-permute-start | bytes 786440 | tf_op jit(solution)/shard_map/ppermute | solution.py:159
  11.6 5.4 %collective-permute-start.7 = (bf16[16,8192]{1,0:T(8,128)(2,1)S(1)}, bf16[16,8192]{1,0:T(8,128)(2,1)S(1)}, u32[]{:S(2)}, u32[]{:S(2)}) collective-permute-start(bf16[16,8192]{1,0:T(8,128)(2,1)S(1)} %collective-permute-done.1.refs_2_), channel_id=1, source_target_pairs={{4,8},{6,10},{8,12},{10,14},{5,9},{7,11},{9,13},{11,15},{20,24},{2... | collective-permute-start | bytes 786440 | tf_op jit(solution)/shard_map/ppermute | solution.py:159
  15.7 8.9 %collective-permute-start.3 = (bf16[16,8192]{1,0:T(8,128)(2,1)S(1)}, bf16[16,8192]{1,0:T(8,128)(2,1)S(1)}, u32[]{:S(2)}, u32[]{:S(2)}) collective-permute-start(bf16[16,8192]{1,0:T(8,128)(2,1)S(1)} %collective-permute-done.2.refs_11_), channel_id=1, source_target_pairs={{4,0},{6,2},{8,4},{10,6},{5,1},{7,3},{9,5},{11,7},{20,16},{22,18},... | collective-permute-start | bytes 786440 | tf_op jit(solution)/shard_map/ppermute | solution.py:159
  17.0 8.9 %collective-permute-start.10 = (bf16[16,8192]{1,0:T(8,128)(2,1)S(1)}, bf16[16,8192]{1,0:T(8,128)(2,1)S(1)}, u32[]{:S(2)}, u32[]{:S(2)}) collective-permute-start(bf16[16,8192]{1,0:T(8,128)(2,1)S(1)} %collective-permute-done.7.refs_6_), channel_id=1, source_target_pairs={{8,12},{10,14},{9,13},{11,15},{24,28},{26,30},{25,29},{27,31}} | collective-permute-start | bytes 786440 | tf_op jit(solution)/shard_map/ppermute | solution.py:159
  24.6 8.3 %collective-permute-start.4 = (bf16[16,8192]{1,0:T(8,128)(2,1)S(1)}, bf16[16,8192]{1,0:T(8,128)(2,1)S(1)}, u32[]{:S(2)}, u32[]{:S(2)}) collective-permute-start(bf16[16,8192]{1,0:T(8,128)(2,1)S(1)} %collective-permute-done.3.refs_7_), channel_id=1, source_target_pairs={{4,0},{6,2},{5,1},{7,3},{20,16},{22,18},{21,17},{23,19}} | collective-permute-start | bytes 786440 | tf_op jit(solution)/shard_map/ppermute | solution.py:159
  32.9 41.5 %all-to-all-start = ((bf16[8,128,256]{2,1,0:T(8,128)(2,1)}), bf16[8,128,256]{2,1,0:T(8,128)(2,1)S(1)}, u32[]{:S(2)}, u32[]{:S(2)}) async-start(bf16[8,128,256]{2,1,0:T(8,128)(2,1)} %param.15), calls=%async_computation | async-start | bytes 1048576 | tf_op jit(solution)/shard_map/all_to_all | solution.py:270
  36.4 13.5 %collective-permute-start = (bf16[16,8192]{1,0:T(8,128)(2,1)S(1)}, bf16[16,8192]{1,0:T(8,128)(2,1)S(1)}, u32[]{:S(2)}, u32[]{:S(2)}) collective-permute-start(bf16[16,8192]{1,0:T(8,128)(2,1)S(1)} %reshape.10.refs_0_), channel_id=1, source_target_pairs={{0,2},{2,0},{4,6},{6,4},{8,10},{10,8},{12,14},{14,12},{1,3},{3,1},... | collective-permute-start | bytes 786440 | tf_op jit(solution)/shard_map/ppermute | solution.py:164
  38.3 17.2 %collective-permute-start.12 = (bf16[16,8192]{1,0:T(8,128)(2,1)S(1)}, bf16[16,8192]{1,0:T(8,128)(2,1)S(1)}, u32[]{:S(2)}, u32[]{:S(2)}) collective-permute-start(bf16[16,8192]{1,0:T(8,128)(2,1)S(1)} %collective-permute-done.2.refs_11_), channel_id=1, source_target_pairs={{0,2},{2,0},{4,6},{6,4},{8,10},{10,8},{1,3},{3,1},{5,7},{7,5},{9,1... | collective-permute-start | bytes 786440 | tf_op jit(solution)/shard_map/ppermute | solution.py:164
  40.4 17.7 %collective-permute-start.5 = (bf16[16,8192]{1,0:T(8,128)(2,1)S(1)}, bf16[16,8192]{1,0:T(8,128)(2,1)S(1)}, u32[]{:S(2)}, u32[]{:S(2)}) collective-permute-start(bf16[16,8192]{1,0:T(8,128)(2,1)S(1)} %collective-permute-done.1.refs_2_), channel_id=1, source_target_pairs={{4,6},{6,4},{8,10},{10,8},{12,14},{14,12},{5,7},{7,5},{9,11},{11,9... | collective-permute-start | bytes 786440 | tf_op jit(solution)/shard_map/ppermute | solution.py:164
  41.1 17.1 %collective-permute-start.8 = (bf16[16,8192]{1,0:T(8,128)(2,1)S(1)}, bf16[16,8192]{1,0:T(8,128)(2,1)S(1)}, u32[]{:S(2)}, u32[]{:S(2)}) collective-permute-start(bf16[16,8192]{1,0:T(8,128)(2,1)S(1)} %collective-permute-done.7.refs_6_), channel_id=1, source_target_pairs={{8,10},{10,8},{12,14},{14,12},{9,11},{11,9},{13,15},{15,13},{24,26... | collective-permute-start | bytes 786440 | tf_op jit(solution)/shard_map/ppermute | solution.py:164
  41.7 19.5 %collective-permute-start.9 = (bf16[16,8192]{1,0:T(8,128)(2,1)S(1)}, bf16[16,8192]{1,0:T(8,128)(2,1)}, u32[]{:S(2)}, u32[]{:S(2)}) collective-permute-start(bf16[16,8192]{1,0:T(8,128)(2,1)S(1)} %collective-permute-done.3.refs_7_), channel_id=1, source_target_pairs={{0,2},{2,0},{4,6},{6,4},{1,3},{3,1},{5,7},{7,5},{16,18},{18,16},{2... | collective-permute-start | bytes 786440 | tf_op jit(solution)/shard_map/ppermute | solution.py:164
  49.9 11.3 %collective-permute-start.11 = (bf16[16,8192]{1,0:T(8,128)(2,1)S(1)}, bf16[16,8192]{1,0:T(8,128)(2,1)}, u32[]{:S(2)}, u32[]{:S(2)}) collective-permute-start(bf16[16,8192]{1,0:T(8,128)(2,1)S(1)} %collective-permute-done.10.refs_10_), channel_id=1, source_target_pairs={{12,14},{14,12},{13,15},{15,13},{28,30},{30,28},{29,31},{31,29}} | collective-permute-start | bytes 786440 | tf_op jit(solution)/shard_map/ppermute | solution.py:164
  55.5 8.6 %collective-permute-start.6 = (bf16[16,8192]{1,0:T(8,128)(2,1)S(1)}, bf16[16,8192]{1,0:T(8,128)(2,1)}, u32[]{:S(2)}, u32[]{:S(2)}) collective-permute-start(bf16[16,8192]{1,0:T(8,128)(2,1)S(1)} %collective-permute-done.4.refs_3_), channel_id=1, source_target_pairs={{0,2},{2,0},{1,3},{3,1},{16,18},{18,16},{17,19},{19,17}} | collective-permute-start | bytes 786440 | tf_op jit(solution)/shard_map/ppermute | solution.py:164
  58.1 20.9 %copy-start.1 = (s32[8,2]{0,1:T(2,128)S(1)}, s32[8,2]{0,1:T(2,128)}, u32[]{:S(2)}) copy-start(s32[8,2]{0,1:T(2,128)} %param.12) | copy-start | bytes 196
  58.1 29.5 %copy-start = (s32[8]{0:T(128)S(1)}, s32[8]{0:T(128)}, u32[]{:S(2)}) copy-start(s32[8]{0:T(128)} %lens_ref.1) | copy-start | bytes 100
  74.4 13.3 %all-to-all-start.1 = ((bf16[8,16,1280]{2,1,0:T(8,128)(2,1)}), bf16[8,16,1280]{2,1,0:T(8,128)(2,1)S(1)}, u32[]{:S(2)}, u32[]{:S(2)}) async-start(bf16[8,16,1280]{2,1,0:T(8,128)(2,1)} %project.1), calls=%async_computation.1 | async-start | bytes 655360 | tf_op jit(solution)/shard_map/all_to_all | solution.py:273
where the time goes:
time: 98.1 us; the launch traced here: 97.6 us
  waiting for transfers between devices  44 us (45%)
  starting transfers between devices  31.1 us (32%)
  Pallas kernels  19.3 us (20%)
  local copies, waits for them, and re-layouts  2.28 us (2%)
    ppermute x6, waiting for transfers between devices, hop(): lax.ppermute(x, axis, [(2 * c + p, 2 * (c + step) + p) for c in range(fir...  21.6 us
    ppermute x7, waiting for transfers between devices, swap(): lax.ppermute(x, axis, [(2 * c + p, 2 * c + 1 - p) for c in range(first, l...  14.6 us
    ppermute x7, starting transfers between devices, swap(): lax.ppermute(x, axis, [(2 * c + p, 2 * c + 1 - p) for c in range(first, l...  12.8 us
    pallas_call x1, Pallas kernels, project(): pl.pallas_call(functools.partial(project_kernel, tiles=tiles, counts=coun...  10.2 us
    ppermute x6, starting transfers between devices, hop(): lax.ppermute(x, axis, [(2 * c + p, 2 * (c + step) + p) for c in range(fir...  10.2 us
    pallas_call x1, Pallas kernels, attend(): pl.pallas_call(kernel, out_shape=jax.ShapeDtypeStruct((tokens, QUERY_HEAD...  9.06 us
    all_to_all x1, waiting for transfers between devices, per_device(): lax.all_to_all(joined, 'tensor', split_axis=0, concat_axis=0, tiled=True)  7.84 us
    all_to_all x1, starting transfers between devices, per_device(): lax.all_to_all(joined, 'tensor', split_axis=0, concat_axis=0, tiled=True)  4.62 us
  transfers between devices with their start and end apart: 15, of which 9 were waited for; matrix products, arithmetic and copies ran while one was open for 0% of the time, Pallas kernels for 10%

commit v1 on v0

--- a/solution.py
+++ b/solution.py
@@ -15,19 +15,27 @@
 STEPS = 2
 MASKED = -1e30
 PROJECT_LIMIT = 48 << 20
+AHEAD = 2
+PAGES_AHEAD = 3
+UNROLL = 1
 ATTEND_LIMIT = 52 << 20
 
 
 def attend_kernel(
     table_ref, lens_ref, slot_ref, q_ref, kv_ref, prompt_ref, pool_ref, out_ref,
-    pages, q_all, acc, top_all, sum_all, q_f32, sems, *, seqs, q_width, kv_off, kv_width, prompt_width,
+    pages, q_pairs, new_scores, new_weights, acc, top_all, sum_all, q_f32, sems,
+    *, seqs, q_width, kv_off, kv_width, prompt_width,
 ):
     span_pages = table_ref.shape[0] // seqs
     page_rows = pool_ref.shape[1]
     span = span_pages * page_rows
     rows = STEPS * GROUP
+    new_rows = seqs * STEPS
     all_rows = KEY_VALUE_HEADS * rows
+    pairs = KEY_VALUE_HEADS // 2
+    wide = 2 * HEAD_SIZE
     value_at = KEY_VALUE_HEADS * HEAD_SIZE
+    heads = range(KEY_VALUE_HEADS)
 
     def page_copy(s, p):
         return pltpu.make_async_copy(
@@ -36,23 +44,17 @@
             sems.at[s, p],
         )
 
-    for s in range(seqs):
+    for s in range(min(PAGES_AHEAD, seqs)):
         for p in range(span_pages):
             page_copy(s, p).start()
 
-    for h in range(QUERY_HEADS):
-        k, g = h // GROUP, h % GROUP
-        block, at = (h * HEAD_SIZE) // q_width, (h * HEAD_SIZE) % q_width
-        q_f32[k, pl.ds(g, seqs * STEPS, stride=GROUP), :] = q_ref[block, :, at : at + HEAD_SIZE].astype(jnp.float32)
-    q_all[...] = q_f32[...].astype(jnp.bfloat16)
-
-    def new_tile(col):
+    def new_pair(col):
         block, at = col // kv_width, kv_off + col % kv_width
-        return kv_ref[block, :, at : at + HEAD_SIZE]
-
-    def prompt_tile(col):
+        return kv_ref[block, :, at : at + wide]
+
+    def prompt_pair(col):
         block, at = col // prompt_width, col % prompt_width
-        return prompt_ref[block, :, at : at + HEAD_SIZE]
+        return prompt_ref[block, :, at : at + wide]
 
     def scaled(q, keys):
         return lax.dot_general(
@@ -62,58 +64,92 @@
     def mix(w, values):
         return jnp.dot(w.astype(jnp.bfloat16), values, preferred_element_type=jnp.float32)
 
+    for h in range(QUERY_HEADS):
+        k, g = h // GROUP, h % GROUP
+        block, at = (h * HEAD_SIZE) // q_width, (h * HEAD_SIZE) % q_width
+        q_f32[k, pl.ds(g, new_rows, stride=GROUP), :] = q_ref[block, :, at : at + HEAD_SIZE].astype(jnp.float32)
+    blank = jnp.zeros((seqs, rows, HEAD_SIZE), jnp.bfloat16)
+    for k in heads:
+        j, half = k // 2, k % 2
+        mine = slice(half * rows, (half + 1) * rows)
+        q_pairs[j, :, mine, half * HEAD_SIZE : (half + 1) * HEAD_SIZE] = (
+            q_f32[k].astype(jnp.bfloat16).reshape(seqs, rows, HEAD_SIZE)
+        )
+        q_pairs[j, :, mine, (1 - half) * HEAD_SIZE : (2 - half) * HEAD_SIZE] = blank
+
+    step_of = (lax.broadcasted_iota(jnp.int32, (seqs, 2 * rows, new_rows), 1) // GROUP) % STEPS
+    seq_of = lax.broadcasted_iota(jnp.int32, (seqs, 2 * rows, new_rows), 0)
+    offset = lax.broadcasted_iota(jnp.int32, (seqs, 2 * rows, new_rows), 2) - seq_of * STEPS
+    live_new = (offset >= 0) & (offset <= step_of)
+    for j in range(pairs):
+        sn = scaled(q_pairs[j].reshape(seqs * 2 * rows, wide), new_pair(j * wide))
+        new_scores[:, j * 2 * rows : (j + 1) * 2 * rows, :] = jnp.where(
+            live_new, sn.reshape(seqs, 2 * rows, new_rows), MASKED
+        )
+
     where_key = lax.broadcasted_iota(jnp.int32, (all_rows, span), 1)
-    step_of = (lax.broadcasted_iota(jnp.int32, (all_rows, seqs * STEPS), 0) // GROUP) % STEPS
-    new_at = lax.broadcasted_iota(jnp.int32, (all_rows, seqs * STEPS), 1)
 
     def one_sequence(s, carry):
+        @pl.when(s + PAGES_AHEAD < seqs)
+        def _():
+            for p in range(span_pages):
+                page_copy(s + PAGES_AHEAD, p).start()
+
         for p in range(span_pages):
             page_copy(s, p).wait()
 
-        def cached(col):
-            return pages[s, :, col : col + HEAD_SIZE]
-
         at = pl.multiple_of(s * rows, rows)
-        q_s = [q_all[k, pl.ds(at, rows), :] for k in range(KEY_VALUE_HEADS)]
         sc = jnp.concatenate(
-            [scaled(q_s[k], cached(k * HEAD_SIZE)) for k in range(KEY_VALUE_HEADS)]
-        )
-        sn = jnp.concatenate([scaled(q_s[k], new_tile(k * HEAD_SIZE)) for k in range(KEY_VALUE_HEADS)])
+            [scaled(q_pairs[j, s], pages[s, :, j * wide : (j + 1) * wide]) for j in range(pairs)]
+        )
         sc = jnp.where(where_key < lens_ref[s], sc, MASKED)
-        offset = new_at - s * STEPS
-        sn = jnp.where((offset >= 0) & (offset <= step_of), sn, MASKED)
+        sn = new_scores[s]
         top = jnp.maximum(jnp.max(sc, axis=1, keepdims=True), jnp.max(sn, axis=1, keepdims=True))
         ec = jnp.exp(sc - top)
         en = jnp.exp(sn - top)
         total = jnp.sum(ec, axis=1, keepdims=True) + jnp.sum(en, axis=1, keepdims=True)
-        for k in range(KEY_VALUE_HEADS):
+        new_weights[s] = en.astype(jnp.bfloat16)
+        for j in range(pairs):
+            col = value_at + j * wide
+            both = mix(ec[j * 2 * rows : (j + 1) * 2 * rows], pages[s, :, col : col + wide])
+            acc[2 * j, pl.ds(at, rows), :] = both[:rows, :HEAD_SIZE]
+            acc[2 * j + 1, pl.ds(at, rows), :] = both[rows:, HEAD_SIZE:]
+        for k in heads:
             part = slice(k * rows, (k + 1) * rows)
-            col = value_at + k * HEAD_SIZE
-            acc[k, pl.ds(at, rows), :] = mix(ec[part], cached(col)) + mix(
-                en[part], new_tile(col)
-            )
             top_all[k, pl.ds(at, rows), :] = jnp.broadcast_to(top[part], (rows, HEAD_SIZE))
             sum_all[k, pl.ds(at, rows), :] = jnp.broadcast_to(total[part], (rows, HEAD_SIZE))
         return carry
 
-    lax.fori_loop(0, seqs, one_sequence, 0, unroll=False)
-
-    at = pl.multiple_of(slot_ref[0] * rows, rows)
-    for k in range(KEY_VALUE_HEADS):
-        mine = (k, pl.ds(at, rows), slice(None))
-        sp = scaled(q_all[mine], prompt_tile(k * HEAD_SIZE))
-        before = top_all[mine]
-        top = jnp.maximum(before, jnp.max(sp, axis=1, keepdims=True))
-        ep = jnp.exp(sp - top[:, :1])
-        keep = jnp.exp(before - top)
-        sum_all[mine] = sum_all[mine] * keep + jnp.sum(ep, axis=1, keepdims=True)
-        acc[mine] = acc[mine] * keep + mix(ep, prompt_tile(value_at + k * HEAD_SIZE))
+    lax.fori_loop(0, seqs, one_sequence, 0, unroll=UNROLL)
+
+    for j in range(pairs):
+        w = new_weights[:, j * 2 * rows : (j + 1) * 2 * rows, :].reshape(seqs * 2 * rows, new_rows)
+        both = mix(w, new_pair(value_at + j * wide)).reshape(seqs, 2 * rows, wide)
+        acc[2 * j] += both[:, :rows, :HEAD_SIZE].reshape(seqs * rows, HEAD_SIZE)
+        acc[2 * j + 1] += both[:, rows:, HEAD_SIZE:].reshape(seqs * rows, HEAD_SIZE)
+
+    slot = slot_ref[0]
+    mine = pl.ds(pl.multiple_of(slot * rows, rows), rows)
+    sp = jnp.concatenate([scaled(q_pairs[j, slot], prompt_pair(j * wide)) for j in range(pairs)])
+    before = jnp.concatenate([top_all[k, mine, :] for k in heads])
+    top = jnp.maximum(before, jnp.max(sp, axis=1, keepdims=True))
+    ep = jnp.exp(sp - top[:, :1])
+    keep = jnp.exp(before - top)
+    more = jnp.sum(ep, axis=1, keepdims=True)
+    for j in range(pairs):
+        both = mix(ep[j * 2 * rows : (j + 1) * 2 * rows], prompt_pair(value_at + j * wide))
+        for half in (0, 1):
+            k = 2 * j + half
+            part = slice(k * rows, (k + 1) * rows)
+            added = both[half * rows : (half + 1) * rows, half * HEAD_SIZE : (half + 1) * HEAD_SIZE]
+            sum_all[k, mine, :] = sum_all[k, mine, :] * keep[part] + more[part]
+            acc[k, mine, :] = acc[k, mine, :] * keep[part] + added
 
     acc[...] = acc[...] / sum_all[...]
     for h in range(QUERY_HEADS):
         k, g = h // GROUP, h % GROUP
         out_ref[:, h * HEAD_SIZE : (h + 1) * HEAD_SIZE] = acc[
-            k, pl.ds(g, seqs * STEPS, stride=GROUP), :
+            k, pl.ds(g, new_rows, stride=GROUP), :
         ].astype(jnp.bfloat16)
 
 
@@ -123,7 +159,7 @@
     kv_width = width - q_width
     kv_off = q_width
     kv = joined
-    if kv_width % HEAD_SIZE:
+    if kv_width % (2 * HEAD_SIZE):
         kv = joined[:, :, q_width:].transpose(1, 0, 2).reshape(1, tokens, blocks * kv_width)
         prompt = prompt.transpose(1, 0, 2).reshape(1, prompt.shape[1], blocks * kv_width)
         kv_width, kv_off = blocks * kv_width, 0
@@ -141,7 +177,9 @@
         out_specs=vmem,
         scratch_shapes=[
             pltpu.VMEM((seqs, table.shape[1] * pool.shape[1], pool.shape[2]), jnp.bfloat16),
-            pltpu.VMEM((KEY_VALUE_HEADS, rows, HEAD_SIZE), jnp.bfloat16),
+            pltpu.VMEM((KEY_VALUE_HEADS // 2, seqs, 2 * STEPS * GROUP, 2 * HEAD_SIZE), jnp.bfloat16),
+            pltpu.VMEM((seqs, QUERY_HEADS * STEPS, tokens), jnp.float32),
+            pltpu.VMEM((seqs, QUERY_HEADS * STEPS, tokens), jnp.bfloat16),
             big, big, big, big,
             pltpu.SemaphoreType.DMA((seqs, table.shape[1])),
         ],
@@ -213,13 +251,15 @@
     for i, (at, width) in enumerate(tiles):
         source = wq_ref.at[:, pl.ds(at, width)] if at < q_width else wkv_ref.at[:, pl.ds(at - q_width, width)]
         copies.append(pltpu.make_async_copy(source, w_here.at[:, pl.ds(at, width)], w_sems.at[i]))
-    for c in copies:
+    for c in copies[:AHEAD]:
         c.start()
     for j, source in enumerate(firsts):
         fetch(j, source).wait()
 
-    for c, (at, width) in zip(copies, tiles):
-        c.wait()
+    for i, (at, width) in enumerate(tiles):
+        copies[i].wait()
+        if i + AHEAD < len(tiles):
+            copies[i + AHEAD].start()
         cols = slice(at, at + width)
         y = jnp.dot(x_here[...], w_here[:, cols], preferred_element_type=jnp.float32).astype(jnp.bfloat16)
         for j in range(size):

time: 98.1 us -> 95.8 us (0.977)
  Pallas kernels: 19.3 us -> 17 us
    pallas_call x1, Pallas kernels: 9.06 us -> 6.57 us  [attend(): pl.pallas_call(kernel, out_shape=jax.ShapeDtypeStruct((tokens, QUERY_HEAD...]
  transfers between devices with their start and end apart: 15 -> 15, of which waited for: 9 -> 9; matrix products, arithmetic and copies ran while one was open for 0% -> 0% of each run, Pallas kernels for 10% -> 11%
where the time goes in v1:
time: 95.8 us; the launch traced here: 95.3 us
  waiting for transfers between devices  44 us (46%)
  starting transfers between devices  31.1 us (32%)
  Pallas kernels  17 us (18%)
  local copies, waits for them, and re-layouts  2.28 us (2%)
    ppermute x6, waiting for transfers between devices, hop(): lax.ppermute(x, axis, [(2 * c + p, 2 * (c + step) + p) for c in range(fir...  21.6 us
    ppermute x7, waiting for transfers between devices, swap(): lax.ppermute(x, axis, [(2 * c + p, 2 * c + 1 - p) for c in range(first, l...  14.6 us
    ppermute x7, starting transfers between devices, swap(): lax.ppermute(x, axis, [(2 * c + p, 2 * c + 1 - p) for c in range(first, l...  12.8 us
    pallas_call x1, Pallas kernels, project(): pl.pallas_call(functools.partial(project_kernel, tiles=tiles, counts=coun...  10.4 us
    ppermute x6, starting transfers between devices, hop(): lax.ppermute(x, axis, [(2 * c + p, 2 * (c + step) + p) for c in range(fir...  10.2 us
    all_to_all x1, waiting for transfers between devices, per_device(): lax.all_to_all(joined, 'tensor', split_axis=0, concat_axis=0, tiled=True)  7.84 us
    pallas_call x1, Pallas kernels, attend(): pl.pallas_call(kernel, out_shape=jax.ShapeDtypeStruct((tokens, QUERY_HEAD...  6.57 us
    all_to_all x1, starting transfers between devices, per_device(): lax.all_to_all(joined, 'tensor', split_axis=0, concat_axis=0, tiled=True)  4.63 us
  transfers between devices with their start and end apart: 15, of which 9 were waited for; matrix products, arithmetic and copies ran while one was open for 0% of the time, Pallas kernels for 11%

profile of v1, /device:TPU:0, one launch (start us, length us, event | category | flops | bytes accessed | tf_op | source)
XLA Modules:
  0.0 95.3 jit_solution(7655038400605610693)
XLA Ops:
  0.0 1.0 %reshape.10.refs_0_ = bf16[16,8192]{1,0:T(8,128)(2,1)S(1)} reshape(bf16[8,2,8192]{2,1,0:T(2,128)(2,1)} %param.8) | data formatting | bytes 524288 | tf_op jit(solution)/shard_map/reshape | solution.py:307
  1.1 5.0 %collective-permute-start.1 = (bf16[16,8192]{1,0:T(8,128)(2,1)S(1)}, bf16[16,8192]{1,0:T(8,128)(2,1)S(1)}, u32[]{:S(2)}, u32[]{:S(2)}) collective-permute-start(bf16[16,8192]{1,0:T(8,128)(2,1)S(1)} %reshape.10.refs_0_), channel_id=1, source_target_pairs={{0,4},{2,6},{4,8},{6,10},{8,12},{10,14},{1,5},{3,7},{5,9},{7,11},{... | collective-permute-start | bytes 786440 | tf_op jit(solution)/shard_map/ppermute | solution.py:197
  6.0 1.3 %collective-permute-start.2 = (bf16[16,8192]{1,0:T(8,128)(2,1)S(1)}, bf16[16,8192]{1,0:T(8,128)(2,1)S(1)}, u32[]{:S(2)}, u32[]{:S(2)}) collective-permute-start(bf16[16,8192]{1,0:T(8,128)(2,1)S(1)} %reshape.10.refs_0_), channel_id=1, source_target_pairs={{4,0},{6,2},{8,4},{10,6},{12,8},{14,10},{5,1},{7,3},{9,5},{11,7},{... | collective-permute-start | bytes 786440 | tf_op jit(solution)/shard_map/ppermute | solution.py:197
  7.3 4.2 %collective-permute-done.1.refs_2_ = bf16[16,8192]{1,0:T(8,128)(2,1)S(1)} collective-permute-done((bf16[16,8192]{1,0:T(8,128)(2,1)S(1)}, bf16[16,8192]{1,0:T(8,128)(2,1)S(1)}, u32[]{:S(2)}, u32[]{:S(2)}) %collective-permute-start.1) | collective-permute-done | bytes 262176 | tf_op jit(solution)/shard_map/ppermute | solution.py:197
  11.6 0.7 collective-permute-start.7
  12.2 3.5 %collective-permute-done.2.refs_11_ = bf16[16,8192]{1,0:T(8,128)(2,1)S(1)} collective-permute-done((bf16[16,8192]{1,0:T(8,128)(2,1)S(1)}, bf16[16,8192]{1,0:T(8,128)(2,1)S(1)}, u32[]{:S(2)}, u32[]{:S(2)}) %collective-permute-start.2) | collective-permute-done | bytes 262176 | tf_op jit(solution)/shard_map/ppermute | solution.py:197
  15.7 1.3 %collective-permute-start.3 = (bf16[16,8192]{1,0:T(8,128)(2,1)S(1)}, bf16[16,8192]{1,0:T(8,128)(2,1)S(1)}, u32[]{:S(2)}, u32[]{:S(2)}) collective-permute-start(bf16[16,8192]{1,0:T(8,128)(2,1)S(1)} %collective-permute-done.2.refs_11_), channel_id=1, source_target_pairs={{4,0},{6,2},{8,4},{10,6},{5,1},{7,3},{9,5},{11,7},{20,16},{22,18},... | collective-permute-start | bytes 786440 | tf_op jit(solution)/shard_map/ppermute | solution.py:197
  17.0 0.0 collective-permute-done.7.refs_6_
  17.0 0.7 collective-permute-start.10
  17.7 6.9 %collective-permute-done.3.refs_7_ = bf16[16,8192]{1,0:T(8,128)(2,1)S(1)} collective-permute-done((bf16[16,8192]{1,0:T(8,128)(2,1)S(1)}, bf16[16,8192]{1,0:T(8,128)(2,1)S(1)}, u32[]{:S(2)}, u32[]{:S(2)}) %collective-permute-start.3) | collective-permute-done | bytes 262176 | tf_op jit(solution)/shard_map/ppermute | solution.py:197
  24.6 1.3 %collective-permute-start.4 = (bf16[16,8192]{1,0:T(8,128)(2,1)S(1)}, bf16[16,8192]{1,0:T(8,128)(2,1)S(1)}, u32[]{:S(2)}, u32[]{:S(2)}) collective-permute-start(bf16[16,8192]{1,0:T(8,128)(2,1)S(1)} %collective-permute-done.3.refs_7_), channel_id=1, source_target_pairs={{4,0},{6,2},{5,1},{7,3},{20,16},{22,18},{21,17},{23,19}} | collective-permute-start | bytes 786440 | tf_op jit(solution)/shard_map/ppermute | solution.py:197
  25.9 0.0 collective-permute-done.10.refs_10_
  25.9 7.0 %collective-permute-done.4.refs_3_ = bf16[16,8192]{1,0:T(8,128)(2,1)S(1)} collective-permute-done((bf16[16,8192]{1,0:T(8,128)(2,1)S(1)}, bf16[16,8192]{1,0:T(8,128)(2,1)S(1)}, u32[]{:S(2)}, u32[]{:S(2)}) %collective-permute-start.4) | collective-permute-done | bytes 262176 | tf_op jit(solution)/shard_map/ppermute | solution.py:197
  32.9 3.5 %all-to-all-start = ((bf16[8,128,256]{2,1,0:T(8,128)(2,1)}), bf16[8,128,256]{2,1,0:T(8,128)(2,1)S(1)}, u32[]{:S(2)}, u32[]{:S(2)}) async-start(bf16[8,128,256]{2,1,0:T(8,128)(2,1)} %param.15), calls=%async_computation | async-start | bytes 1048576 | tf_op jit(solution)/shard_map/all_to_all | solution.py:310
  36.4 1.9 %collective-permute-start = (bf16[16,8192]{1,0:T(8,128)(2,1)S(1)}, bf16[16,8192]{1,0:T(8,128)(2,1)S(1)}, u32[]{:S(2)}, u32[]{:S(2)}) collective-permute-start(bf16[16,8192]{1,0:T(8,128)(2,1)S(1)} %reshape.10.refs_0_), channel_id=1, source_target_pairs={{0,2},{2,0},{4,6},{6,4},{8,10},{10,8},{12,14},{14,12},{1,3},{3,1},... | collective-permute-start | bytes 786440 | tf_op jit(solution)/shard_map/ppermute | solution.py:202
  38.3 2.1 %collective-permute-start.12 = (bf16[16,8192]{1,0:T(8,128)(2,1)S(1)}, bf16[16,8192]{1,0:T(8,128)(2,1)S(1)}, u32[]{:S(2)}, u32[]{:S(2)}) collective-permute-start(bf16[16,8192]{1,0:T(8,128)(2,1)S(1)} %collective-permute-done.2.refs_11_), channel_id=1, source_target_pairs={{0,2},{2,0},{4,6},{6,4},{8,10},{10,8},{1,3},{3,1},{5,7},{7,5},{9,1... | collective-permute-start | bytes 786440 | tf_op jit(solution)/shard_map/ppermute | solution.py:202
  40.4 0.7 collective-permute-start.5
  41.1 0.7 collective-permute-start.8
  41.7 3.8 %collective-permute-start.9 = (bf16[16,8192]{1,0:T(8,128)(2,1)S(1)}, bf16[16,8192]{1,0:T(8,128)(2,1)}, u32[]{:S(2)}, u32[]{:S(2)}) collective-permute-start(bf16[16,8192]{1,0:T(8,128)(2,1)S(1)} %collective-permute-done.3.refs_7_), channel_id=1, source_target_pairs={{0,2},{2,0},{4,6},{6,4},{1,3},{3,1},{5,7},{7,5},{16,18},{18,16},{2... | collective-permute-start | bytes 786440 | tf_op jit(solution)/shard_map/ppermute | solution.py:202
  45.5 4.4 %collective-permute-done.refs_1_ = bf16[16,8192]{1,0:T(8,128)(2,1)S(1)} collective-permute-done((bf16[16,8192]{1,0:T(8,128)(2,1)S(1)}, bf16[16,8192]{1,0:T(8,128)(2,1)S(1)}, u32[]{:S(2)}, u32[]{:S(2)}) %collective-permute-start) | collective-permute-done | bytes 262176 | tf_op jit(solution)/shard_map/ppermute | solution.py:202
  49.9 1.4 %collective-permute-start.11 = (bf16[16,8192]{1,0:T(8,128)(2,1)S(1)}, bf16[16,8192]{1,0:T(8,128)(2,1)}, u32[]{:S(2)}, u32[]{:S(2)}) collective-permute-start(bf16[16,8192]{1,0:T(8,128)(2,1)S(1)} %collective-permute-done.10.refs_10_), channel_id=1, source_target_pairs={{12,14},{14,12},{13,15},{15,13},{28,30},{30,28},{29,31},{31,29}} | collective-permute-start | bytes 786440 | tf_op jit(solution)/shard_map/ppermute | solution.py:202
  51.2 4.3 %collective-permute-done.12.refs_13_ = bf16[16,8192]{1,0:T(8,128)(2,1)S(1)} collective-permute-done((bf16[16,8192]{1,0:T(8,128)(2,1)S(1)}, bf16[16,8192]{1,0:T(8,128)(2,1)S(1)}, u32[]{:S(2)}, u32[]{:S(2)}) %collective-permute-start.12) | collective-permute-done | bytes 262176 | tf_op jit(solution)/shard_map/ppermute | solution.py:202
  55.5 2.3 %collective-permute-start.6 = (bf16[16,8192]{1,0:T(8,128)(2,1)S(1)}, bf16[16,8192]{1,0:T(8,128)(2,1)}, u32[]{:S(2)}, u32[]{:S(2)}) collective-permute-start(bf16[16,8192]{1,0:T(8,128)(2,1)S(1)} %collective-permute-done.4.refs_3_), channel_id=1, source_target_pairs={{0,2},{2,0},{1,3},{3,1},{16,18},{18,16},{17,19},{19,17}} | collective-permute-start | bytes 786440 | tf_op jit(solution)/shard_map/ppermute | solution.py:202
  57.9 0.1 stack.54.choice_ref
  58.0 0.1 stack.50.owner_ref
  58.1 0.0 copy-start.1
  58.1 0.0 copy-start
  58.1 0.0 collective-permute-done.5.refs_4_
  58.1 0.0 collective-permute-done.8.refs_8_
  58.1 3.1 %collective-permute-done.9.refs_9_ = bf16[16,8192]{1,0:T(8,128)(2,1)} collective-permute-done((bf16[16,8192]{1,0:T(8,128)(2,1)S(1)}, bf16[16,8192]{1,0:T(8,128)(2,1)}, u32[]{:S(2)}, u32[]{:S(2)}) %collective-permute-start.9) | collective-permute-done | bytes 262176 | tf_op jit(solution)/shard_map/ppermute | solution.py:202
  61.2 0.0 collective-permute-done.11.refs_12_
  61.2 2.9 %collective-permute-done.6.refs_5_ = bf16[16,8192]{1,0:T(8,128)(2,1)} collective-permute-done((bf16[16,8192]{1,0:T(8,128)(2,1)S(1)}, bf16[16,8192]{1,0:T(8,128)(2,1)}, u32[]{:S(2)}, u32[]{:S(2)}) %collective-permute-start.6) | collective-permute-done | bytes 262176 | tf_op jit(solution)/shard_map/ppermute | solution.py:202
  64.1 10.4 %project.1 = bf16[8,16,1280]{2,1,0:T(8,128)(2,1)} custom-call(s32[8]{0:T(128)S(1)} %stack.50.owner_ref, s32[8]{0:T(128)S(1)} %stack.54.choice_ref, bf16[16,8192]{1,0:T(8,128)(2,1)S(1)} %reshape.10.refs_0_, bf16[16,8192]{1,0:T(8,128)(2,1)S(1)} %collective-permute-done.refs_1_, bf16[16,8192]{1,0:T(8,128)(2,1)S(1)} %collective-permute-done.1.refs_2_, ...), custom_call_target="tpu_custom_call" | custom-call | flops 2684354560 | bytes 23068672 | tf_op jit(solution)/shard_map/project/pallas_call | solution.py:284
  74.5 0.0 all-to-all-done.prompt_ref
  74.5 4.6 %all-to-all-start.1 = ((bf16[8,16,1280]{2,1,0:T(8,128)(2,1)}), bf16[8,16,1280]{2,1,0:T(8,128)(2,1)S(1)}, u32[]{:S(2)}, u32[]{:S(2)}) async-start(bf16[8,16,1280]{2,1,0:T(8,128)(2,1)} %project.1), calls=%async_computation.1 | async-start | bytes 655360 | tf_op jit(solution)/shard_map/all_to_all | solution.py:313
  79.1 0.0 copy-done.1
  79.1 0.1 copy.10
  79.2 0.1 reshape.9.table_ref
  80.0 7.8 %all-to-all-done.1.q_ref.kv_ref = bf16[8,16,1280]{2,1,0:T(8,128)(2,1)S(1)} async-done(((bf16[8,16,1280]{2,1,0:T(8,128)(2,1)}), bf16[8,16,1280]{2,1,0:T(8,128)(2,1)S(1)}, u32[]{:S(2)}, u32[]{:S(2)}) %all-to-all-start.1) | async-done | bytes 327712 | tf_op jit(solution)/shard_map/all_to_all | solution.py:313
  87.8 0.0 copy-done
  87.8 6.6 %attend.1 = bf16[16,8192]{1,0:T(8,128)(2,1)S(1)} custom-call(s32[16]{0:T(128)S(1)} %reshape.9.table_ref, s32[8]{0:T(128)S(1)} %copy-done, s32[1]{0:T(128)S(6)} %copy.11.slot_ref, bf16[8,16,1280]{2,1,0:T(8,128)(2,1)S(1)} %all-to-all-done.1.q_ref.kv_ref, bf16[8,16,1280]{2,1,0:T(8,128)(2,1)S(1)} %all-to-all-done.1.q_ref.kv_ref, ...), custom_call_target="tpu_custom_call" | custom-call | tf_op jit(solution)/shard_map/attend/pallas_call | solution.py:173
  94.4 0.9 reshape.11
  (1 shorter events, 0.0 us)
Async XLA Ops:
  1.1 10.5 %collective-permute-start.1 = (bf16[16,8192]{1,0:T(8,128)(2,1)S(1)}, bf16[16,8192]{1,0:T(8,128)(2,1)S(1)}, u32[]{:S(2)}, u32[]{:S(2)}) collective-permute-start(bf16[16,8192]{1,0:T(8,128)(2,1)S(1)} %reshape.10.refs_0_), channel_id=1, source_target_pairs={{0,4},{2,6},{4,8},{6,10},{8,12},{10,14},{1,5},{3,7},{5,9},{7,11},{... | collective-permute-start | bytes 786440 | tf_op jit(solution)/shard_map/ppermute | solution.py:197
  6.0 9.7 %collective-permute-start.2 = (bf16[16,8192]{1,0:T(8,128)(2,1)S(1)}, bf16[16,8192]{1,0:T(8,128)(2,1)S(1)}, u32[]{:S(2)}, u32[]{:S(2)}) collective-permute-start(bf16[16,8192]{1,0:T(8,128)(2,1)S(1)} %reshape.10.refs_0_), channel_id=1, source_target_pairs={{4,0},{6,2},{8,4},{10,6},{12,8},{14,10},{5,1},{7,3},{9,5},{11,7},{... | collective-permute-start | bytes 786440 | tf_op jit(solution)/shard_map/ppermute | solution.py:197
  11.6 5.4 %collective-permute-start.7 = (bf16[16,8192]{1,0:T(8,128)(2,1)S(1)}, bf16[16,8192]{1,0:T(8,128)(2,1)S(1)}, u32[]{:S(2)}, u32[]{:S(2)}) collective-permute-start(bf16[16,8192]{1,0:T(8,128)(2,1)S(1)} %collective-permute-done.1.refs_2_), channel_id=1, source_target_pairs={{4,8},{6,10},{8,12},{10,14},{5,9},{7,11},{9,13},{11,15},{20,24},{2... | collective-permute-start | bytes 786440 | tf_op jit(solution)/shard_map/ppermute | solution.py:197
  15.7 8.9 %collective-permute-start.3 = (bf16[16,8192]{1,0:T(8,128)(2,1)S(1)}, bf16[16,8192]{1,0:T(8,128)(2,1)S(1)}, u32[]{:S(2)}, u32[]{:S(2)}) collective-permute-start(bf16[16,8192]{1,0:T(8,128)(2,1)S(1)} %collective-permute-done.2.refs_11_), channel_id=1, source_target_pairs={{4,0},{6,2},{8,4},{10,6},{5,1},{7,3},{9,5},{11,7},{20,16},{22,18},... | collective-permute-start | bytes 786440 | tf_op jit(solution)/shard_map/ppermute | solution.py:197
  17.0 8.9 %collective-permute-start.10 = (bf16[16,8192]{1,0:T(8,128)(2,1)S(1)}, bf16[16,8192]{1,0:T(8,128)(2,1)S(1)}, u32[]{:S(2)}, u32[]{:S(2)}) collective-permute-start(bf16[16,8192]{1,0:T(8,128)(2,1)S(1)} %collective-permute-done.7.refs_6_), channel_id=1, source_target_pairs={{8,12},{10,14},{9,13},{11,15},{24,28},{26,30},{25,29},{27,31}} | collective-permute-start | bytes 786440 | tf_op jit(solution)/shard_map/ppermute | solution.py:197
  24.6 8.3 %collective-permute-start.4 = (bf16[16,8192]{1,0:T(8,128)(2,1)S(1)}, bf16[16,8192]{1,0:T(8,128)(2,1)S(1)}, u32[]{:S(2)}, u32[]{:S(2)}) collective-permute-start(bf16[16,8192]{1,0:T(8,128)(2,1)S(1)} %collective-permute-done.3.refs_7_), channel_id=1, source_target_pairs={{4,0},{6,2},{5,1},{7,3},{20,16},{22,18},{21,17},{23,19}} | collective-permute-start | bytes 786440 | tf_op jit(solution)/shard_map/ppermute | solution.py:197
  32.9 41.6 %all-to-all-start = ((bf16[8,128,256]{2,1,0:T(8,128)(2,1)}), bf16[8,128,256]{2,1,0:T(8,128)(2,1)S(1)}, u32[]{:S(2)}, u32[]{:S(2)}) async-start(bf16[8,128,256]{2,1,0:T(8,128)(2,1)} %param.15), calls=%async_computation | async-start | bytes 1048576 | tf_op jit(solution)/shard_map/all_to_all | solution.py:310
  36.4 13.5 %collective-permute-start = (bf16[16,8192]{1,0:T(8,128)(2,1)S(1)}, bf16[16,8192]{1,0:T(8,128)(2,1)S(1)}, u32[]{:S(2)}, u32[]{:S(2)}) collective-permute-start(bf16[16,8192]{1,0:T(8,128)(2,1)S(1)} %reshape.10.refs_0_), channel_id=1, source_target_pairs={{0,2},{2,0},{4,6},{6,4},{8,10},{10,8},{12,14},{14,12},{1,3},{3,1},... | collective-permute-start | bytes 786440 | tf_op jit(solution)/shard_map/ppermute | solution.py:202
  38.3 17.2 %collective-permute-start.12 = (bf16[16,8192]{1,0:T(8,128)(2,1)S(1)}, bf16[16,8192]{1,0:T(8,128)(2,1)S(1)}, u32[]{:S(2)}, u32[]{:S(2)}) collective-permute-start(bf16[16,8192]{1,0:T(8,128)(2,1)S(1)} %collective-permute-done.2.refs_11_), channel_id=1, source_target_pairs={{0,2},{2,0},{4,6},{6,4},{8,10},{10,8},{1,3},{3,1},{5,7},{7,5},{9,1... | collective-permute-start | bytes 786440 | tf_op jit(solution)/shard_map/ppermute | solution.py:202
  40.4 17.7 %collective-permute-start.5 = (bf16[16,8192]{1,0:T(8,128)(2,1)S(1)}, bf16[16,8192]{1,0:T(8,128)(2,1)S(1)}, u32[]{:S(2)}, u32[]{:S(2)}) collective-permute-start(bf16[16,8192]{1,0:T(8,128)(2,1)S(1)} %collective-permute-done.1.refs_2_), channel_id=1, source_target_pairs={{4,6},{6,4},{8,10},{10,8},{12,14},{14,12},{5,7},{7,5},{9,11},{11,9... | collective-permute-start | bytes 786440 | tf_op jit(solution)/shard_map/ppermute | solution.py:202
  41.1 17.1 %collective-permute-start.8 = (bf16[16,8192]{1,0:T(8,128)(2,1)S(1)}, bf16[16,8192]{1,0:T(8,128)(2,1)S(1)}, u32[]{:S(2)}, u32[]{:S(2)}) collective-permute-start(bf16[16,8192]{1,0:T(8,128)(2,1)S(1)} %collective-permute-done.7.refs_6_), channel_id=1, source_target_pairs={{8,10},{10,8},{12,14},{14,12},{9,11},{11,9},{13,15},{15,13},{24,26... | collective-permute-start | bytes 786440 | tf_op jit(solution)/shard_map/ppermute | solution.py:202
  41.7 19.5 %collective-permute-start.9 = (bf16[16,8192]{1,0:T(8,128)(2,1)S(1)}, bf16[16,8192]{1,0:T(8,128)(2,1)}, u32[]{:S(2)}, u32[]{:S(2)}) collective-permute-start(bf16[16,8192]{1,0:T(8,128)(2,1)S(1)} %collective-permute-done.3.refs_7_), channel_id=1, source_target_pairs={{0,2},{2,0},{4,6},{6,4},{1,3},{3,1},{5,7},{7,5},{16,18},{18,16},{2... | collective-permute-start | bytes 786440 | tf_op jit(solution)/shard_map/ppermute | solution.py:202
  49.9 11.3 %collective-permute-start.11 = (bf16[16,8192]{1,0:T(8,128)(2,1)S(1)}, bf16[16,8192]{1,0:T(8,128)(2,1)}, u32[]{:S(2)}, u32[]{:S(2)}) collective-permute-start(bf16[16,8192]{1,0:T(8,128)(2,1)S(1)} %collective-permute-done.10.refs_10_), channel_id=1, source_target_pairs={{12,14},{14,12},{13,15},{15,13},{28,30},{30,28},{29,31},{31,29}} | collective-permute-start | bytes 786440 | tf_op jit(solution)/shard_map/ppermute | solution.py:202
  55.5 8.6 %collective-permute-start.6 = (bf16[16,8192]{1,0:T(8,128)(2,1)S(1)}, bf16[16,8192]{1,0:T(8,128)(2,1)}, u32[]{:S(2)}, u32[]{:S(2)}) collective-permute-start(bf16[16,8192]{1,0:T(8,128)(2,1)S(1)} %collective-permute-done.4.refs_3_), channel_id=1, source_target_pairs={{0,2},{2,0},{1,3},{3,1},{16,18},{18,16},{17,19},{19,17}} | collective-permute-start | bytes 786440 | tf_op jit(solution)/shard_map/ppermute | solution.py:202
  58.1 21.0 %copy-start.1 = (s32[8,2]{0,1:T(2,128)S(1)}, s32[8,2]{0,1:T(2,128)}, u32[]{:S(2)}) copy-start(s32[8,2]{0,1:T(2,128)} %param.12) | copy-start | bytes 196
  58.1 29.7 %copy-start = (s32[8]{0:T(128)S(1)}, s32[8]{0:T(128)}, u32[]{:S(2)}) copy-start(s32[8]{0:T(128)} %lens_ref.1) | copy-start | bytes 100
  74.5 13.3 %all-to-all-start.1 = ((bf16[8,16,1280]{2,1,0:T(8,128)(2,1)}), bf16[8,16,1280]{2,1,0:T(8,128)(2,1)S(1)}, u32[]{:S(2)}, u32[]{:S(2)}) async-start(bf16[8,16,1280]{2,1,0:T(8,128)(2,1)} %project.1), calls=%async_computation.1 | async-start | bytes 655360 | tf_op jit(solution)/shard_map/all_to_all | solution.py:313

commit v2 on v1

--- a/solution.py
+++ b/solution.py
@@ -17,18 +17,20 @@
 PROJECT_LIMIT = 48 << 20
 AHEAD = 2
 PAGES_AHEAD = 3
-UNROLL = 1
-ATTEND_LIMIT = 52 << 20
+EARLY = 2
+EARLY_LIMIT = 50 << 20
+ATTEND_LIMIT = 50 << 20
 
 
 def attend_kernel(
-    table_ref, lens_ref, slot_ref, q_ref, kv_ref, prompt_ref, pool_ref, out_ref,
+    table_ref, lens_ref, slot_ref, q_ref, kv_ref, prompt_ref, early_ref, pool_ref, out_ref,
     pages, q_pairs, new_scores, new_weights, acc, top_all, sum_all, q_f32, sems,
     *, seqs, q_width, kv_off, kv_width, prompt_width,
 ):
     span_pages = table_ref.shape[0] // seqs
     page_rows = pool_ref.shape[1]
     span = span_pages * page_rows
+    early = early_ref.shape[0]
     rows = STEPS * GROUP
     new_rows = seqs * STEPS
     all_rows = KEY_VALUE_HEADS * rows
@@ -40,11 +42,11 @@
     def page_copy(s, p):
         return pltpu.make_async_copy(
             pool_ref.at[table_ref[s * span_pages + p]],
-            pages.at[s, pl.ds(p * page_rows, page_rows)],
-            sems.at[s, p],
-        )
-
-    for s in range(min(PAGES_AHEAD, seqs)):
+            pages.at[s - early, pl.ds(p * page_rows, page_rows)],
+            sems.at[s - early, p],
+        )
+
+    for s in range(early, min(early + PAGES_AHEAD, seqs)):
         for p in range(span_pages):
             page_copy(s, p).start()
 
@@ -89,18 +91,10 @@
 
     where_key = lax.broadcasted_iota(jnp.int32, (all_rows, span), 1)
 
-    def one_sequence(s, carry):
-        @pl.when(s + PAGES_AHEAD < seqs)
-        def _():
-            for p in range(span_pages):
-                page_copy(s + PAGES_AHEAD, p).start()
-
-        for p in range(span_pages):
-            page_copy(s, p).wait()
-
+    def one_sequence(s, context):
         at = pl.multiple_of(s * rows, rows)
         sc = jnp.concatenate(
-            [scaled(q_pairs[j, s], pages[s, :, j * wide : (j + 1) * wide]) for j in range(pairs)]
+            [scaled(q_pairs[j, s], context[:, j * wide : (j + 1) * wide]) for j in range(pairs)]
         )
         sc = jnp.where(where_key < lens_ref[s], sc, MASKED)
         sn = new_scores[s]
@@ -111,16 +105,28 @@
         new_weights[s] = en.astype(jnp.bfloat16)
         for j in range(pairs):
             col = value_at + j * wide
-            both = mix(ec[j * 2 * rows : (j + 1) * 2 * rows], pages[s, :, col : col + wide])
+            both = mix(ec[j * 2 * rows : (j + 1) * 2 * rows], context[:, col : col + wide])
             acc[2 * j, pl.ds(at, rows), :] = both[:rows, :HEAD_SIZE]
             acc[2 * j + 1, pl.ds(at, rows), :] = both[rows:, HEAD_SIZE:]
         for k in heads:
             part = slice(k * rows, (k + 1) * rows)
             top_all[k, pl.ds(at, rows), :] = jnp.broadcast_to(top[part], (rows, HEAD_SIZE))
             sum_all[k, pl.ds(at, rows), :] = jnp.broadcast_to(total[part], (rows, HEAD_SIZE))
-        return carry
-
-    lax.fori_loop(0, seqs, one_sequence, 0, unroll=UNROLL)
+
+    @pl.loop(0, early)
+    def _(s):
+        one_sequence(s, early_ref.at[s])
+
+    @pl.loop(early, seqs)
+    def _(s):
+        @pl.when(s + PAGES_AHEAD < seqs)
+        def _():
+            for p in range(span_pages):
+                page_copy(s + PAGES_AHEAD, p).start()
+
+        for p in range(span_pages):
+            page_copy(s, p).wait()
+        one_sequence(s, pages.at[s - early])
 
     for j in range(pairs):
         w = new_weights[:, j * 2 * rows : (j + 1) * 2 * rows, :].reshape(seqs * 2 * rows, new_rows)
@@ -148,12 +154,11 @@
     acc[...] = acc[...] / sum_all[...]
     for h in range(QUERY_HEADS):
         k, g = h // GROUP, h % GROUP
-        out_ref[:, h * HEAD_SIZE : (h + 1) * HEAD_SIZE] = acc[
-            k, pl.ds(g, new_rows, stride=GROUP), :
-        ].astype(jnp.bfloat16)
-
-
-def attend(joined, q_width, prompt, pool, table, lens, slot):
+        head = acc[k, pl.ds(g, new_rows, stride=GROUP), :].astype(jnp.bfloat16)
+        out_ref[:, :, h * HEAD_SIZE : (h + 1) * HEAD_SIZE] = head.reshape(seqs, STEPS, HEAD_SIZE)
+
+
+def attend(joined, q_width, prompt, early, pool, table, lens, slot):
     blocks, tokens, width = joined.shape
     seqs = tokens // STEPS
     kv_width = width - q_width
@@ -172,20 +177,52 @@
     big = pltpu.VMEM((KEY_VALUE_HEADS, rows, HEAD_SIZE), jnp.float32)
     return pl.pallas_call(
         kernel,
-        out_shape=jax.ShapeDtypeStruct((tokens, QUERY_HEADS * HEAD_SIZE), jnp.bfloat16),
-        in_specs=[smem, smem, smem, vmem, vmem, vmem, pl.BlockSpec(memory_space=pl.ANY)],
+        out_shape=jax.ShapeDtypeStruct((seqs, STEPS, QUERY_HEADS * HEAD_SIZE), jnp.bfloat16),
+        in_specs=[smem, smem, smem, vmem, vmem, vmem, vmem, pl.BlockSpec(memory_space=pl.ANY)],
         out_specs=vmem,
         scratch_shapes=[
-            pltpu.VMEM((seqs, table.shape[1] * pool.shape[1], pool.shape[2]), jnp.bfloat16),
+            pltpu.VMEM((seqs - early.shape[0], table.shape[1] * pool.shape[1], pool.shape[2]), jnp.bfloat16),
             pltpu.VMEM((KEY_VALUE_HEADS // 2, seqs, 2 * STEPS * GROUP, 2 * HEAD_SIZE), jnp.bfloat16),
             pltpu.VMEM((seqs, QUERY_HEADS * STEPS, tokens), jnp.float32),
             pltpu.VMEM((seqs, QUERY_HEADS * STEPS, tokens), jnp.bfloat16),
             big, big, big, big,
-            pltpu.SemaphoreType.DMA((seqs, table.shape[1])),
+            pltpu.SemaphoreType.DMA((seqs - early.shape[0], table.shape[1])),
         ],
         compiler_params=pltpu.CompilerParams(vmem_limit_bytes=ATTEND_LIMIT),
         name="attend",
-    )(table.reshape(-1), lens, slot, joined, kv, prompt, pool)
+    )(table.reshape(-1), lens, slot, joined, kv, prompt, early, pool)
+
+
+def early_kernel(table_ref, token_ref, pool_ref, out_ref, sems):
+    page_rows = pool_ref.shape[1]
+    each = out_ref.shape[1] // page_rows
+    copies = [
+        pltpu.make_async_copy(
+            pool_ref.at[table_ref[s * each + p]], out_ref.at[s, pl.ds(p * page_rows, page_rows)], sems.at[s, p]
+        )
+        for s in range(out_ref.shape[0])
+        for p in range(each)
+    ]
+    for c in copies:
+        c.start()
+    for c in copies:
+        c.wait()
+
+
+def early_pages(token, table, pool):
+    seqs, each = min(EARLY, table.shape[0]), table.shape[1]
+    hbm = pl.BlockSpec(memory_space=pl.ANY)
+    shape = (seqs, each * pool.shape[1], pool.shape[2])
+    return pl.pallas_call(
+        early_kernel,
+        out_shape=pltpu.VMEM(shape, pool.dtype),
+        in_specs=[pl.BlockSpec(memory_space=pltpu.SMEM), hbm, hbm],
+        out_specs=pl.BlockSpec(memory_space=pltpu.VMEM),
+        scratch_shapes=[pltpu.SemaphoreType.DMA((seqs, each))],
+        compiler_params=pltpu.CompilerParams(vmem_limit_bytes=EARLY_LIMIT),
+        cost_estimate=pl.CostEstimate(flops=0, bytes_accessed=4 * shape[0] * shape[1] * shape[2], transcendentals=0),
+        name="early",
+    )(table.reshape(-1), token, pool)
 
 
 def gather_blocks(own, axis, size):
@@ -205,11 +242,21 @@
     up_pair, down_pair = {}, {}
     near = swap(own, 0, line - 1)
     found = [((own,), 0, me), ((near,), 0, 2 * place + 1 - side)]
-    for s in range(1, line):
+    for s in range(1, line - 1):
         up[s] = hop(up[s - 1], 1, s - 1, line - 2)
         down[s] = hop(down[s - 1], -1, 1, line - s)
-        up_pair[s] = swap(up[s], s, line - 1)
-        down_pair[s] = swap(down[s], 0, line - 1 - s)
+        if s < line - 2:
+            up_pair[s] = swap(up[s], s, line - 1)
+            down_pair[s] = swap(down[s], 0, line - 1 - s)
+    both = jnp.where(2 * place >= line, up[line - 2], down[line - 2])
+    ends = [(1, 0), (line - 2, line - 1)]
+    up[line - 1] = down[line - 1] = lax.ppermute(both, axis, [(2 * a + p, 2 * b + p) for a, b in ends for p in (0, 1)])
+    up_pair[line - 2] = down_pair[line - 2] = lax.ppermute(
+        both, axis, [(2 * c + p, 2 * c + 1 - p) for c in (0, 1, line - 2, line - 1) for p in (0, 1)]
+    )
+    up_pair[line - 1] = down_pair[line - 1] = lax.ppermute(
+        up[line - 1], axis, [(2 * c + p, 2 * c + 1 - p) for c in (0, line - 1) for p in (0, 1)]
+    )
     for s in range(1, line):
         other = (place + line - s) % line
         first = place >= s
@@ -311,8 +358,8 @@
     joined = project(found, wq, wkv)
     joined, prompt = lax.optimization_barrier((joined, prompt))
     back = lax.all_to_all(joined, "tensor", split_axis=0, concat_axis=0, tiled=True)
-    out = attend(back, wq.shape[1], prompt, cache_pool, page_table, ctx_len, prompt_slot)
-    return out.reshape(hidden.shape[0], hidden.shape[1], -1)
+    early = early_pages(joined, page_table, cache_pool)
+    return attend(back, wq.shape[1], prompt, early, cache_pool, page_table, ctx_len, prompt_slot)
 
 
 def solution(mesh):

time: 95.8 us -> 95.5 us (level)
  starting transfers between devices: 31.1 us -> 26.2 us
  waiting for transfers between devices: 44 us -> 46.9 us
  Pallas kernels: 17 us -> 18.9 us
    ppermute x0 -> x3, waiting for transfers between devices: none -> 15.7 us  [the longest x1 7.18 us: gather_blocks(): lax.ppermute(both, axis, [(2 * a + p, 2 * b + p) for a, b in ends for p i...]
    ppermute x7 -> x3, starting transfers between devices: 12.8 us -> 4.66 us  [swap(): lax.ppermute(x, axis, [(2 * c + p, 2 * c + 1 - p) for c in range(first, l...]
    ppermute x6 -> x4, waiting for transfers between devices: 21.6 us -> 15.3 us  [hop(): lax.ppermute(x, axis, [(2 * c + p, 2 * (c + step) + p) for c in range(fir...]
    ppermute x0 -> x3, starting transfers between devices: none -> 5.27 us  [the longest x1 2.07 us: gather_blocks(): lax.ppermute(up[line - 1], axis, [(2 * c + p, 2 * c + 1 - p) for c in (0,...]
    ppermute x7 -> x3, waiting for transfers between devices: 14.6 us -> 10.2 us  [swap(): lax.ppermute(x, axis, [(2 * c + p, 2 * c + 1 - p) for c in range(first, l...]
    all_to_all x1, waiting for transfers between devices: 7.84 us -> 5.74 us  [per_device(): lax.all_to_all(joined, 'tensor', split_axis=0, concat_axis=0, tiled=True)]
    ppermute x6 -> x4, starting transfers between devices: 10.2 us -> 8.21 us  [hop(): lax.ppermute(x, axis, [(2 * c + p, 2 * (c + step) + p) for c in range(fir...]
    pallas_call x1 -> x2, Pallas kernels: 6.57 us -> 8.5 us  [the longest x1 6.4 us: attend(): pl.pallas_call(kernel, out_shape=jax.ShapeDtypeStruct((seqs, STEPS, QUERY...]
  transfers between devices with their start and end apart: 15 -> 12, of which waited for: 9 -> 9; matrix products, arithmetic and copies ran while one was open for 0% -> 0% of each run, Pallas kernels for 11% -> 13%
where the time goes in v2:
time: 95.5 us; the launch traced here: 95 us
  waiting for transfers between devices  46.9 us (49%)
  starting transfers between devices  26.2 us (27%)
  Pallas kernels  18.9 us (20%)
  local copies, waits for them, and re-layouts  1.4 us (1%)
    ppermute x4, waiting for transfers between devices, hop(): lax.ppermute(x, axis, [(2 * c + p, 2 * (c + step) + p) for c in range(fir...  15.3 us
    pallas_call x1, Pallas kernels, project(): pl.pallas_call(functools.partial(project_kernel, tiles=tiles, counts=coun...  10.4 us
    ppermute x3, waiting for transfers between devices, swap(): lax.ppermute(x, axis, [(2 * c + p, 2 * c + 1 - p) for c in range(first, l...  10.2 us
    ppermute x4, starting transfers between devices, hop(): lax.ppermute(x, axis, [(2 * c + p, 2 * (c + step) + p) for c in range(fir...  8.21 us
    ppermute x1, waiting for transfers between devices, gather_blocks(): lax.ppermute(both, axis, [(2 * a + p, 2 * b + p) for a, b in ends for p i...  7.18 us
    pallas_call x1, Pallas kernels, attend(): pl.pallas_call(kernel, out_shape=jax.ShapeDtypeStruct((seqs, STEPS, QUERY...  6.4 us
    all_to_all x1, waiting for transfers between devices, per_device(): lax.all_to_all(joined, 'tensor', split_axis=0, concat_axis=0, tiled=True)  5.74 us
    ppermute x1, waiting for transfers between devices, gather_blocks(): lax.ppermute(both, axis, [(2 * c + p, 2 * c + 1 - p) for c in (0, 1, line...  5.62 us
  transfers between devices with their start and end apart: 12, of which 9 were waited for; matrix products, arithmetic and copies ran while one was open for 0% of the time, Pallas kernels for 13%

profile of v2, /device:TPU:0, one launch (start us, length us, event | category | flops | bytes accessed | tf_op | source)
XLA Modules:
  0.0 95.0 jit_solution(844227406117819635)
XLA Ops:
  0.0 1.0 %reshape.8.refs_0_ = bf16[16,8192]{1,0:T(8,128)(2,1)S(1)} reshape(bf16[8,2,8192]{2,1,0:T(2,128)(2,1)} %param.8) | data formatting | bytes 524288 | tf_op jit(solution)/shard_map/reshape | solution.py:354
  1.1 5.0 %collective-permute-start.1 = (bf16[16,8192]{1,0:T(8,128)(2,1)S(1)}, bf16[16,8192]{1,0:T(8,128)(2,1)S(1)}, u32[]{:S(2)}, u32[]{:S(2)}) collective-permute-start(bf16[16,8192]{1,0:T(8,128)(2,1)S(1)} %reshape.8.refs_0_), channel_id=1, source_target_pairs={{0,4},{2,6},{4,8},{6,10},{8,12},{10,14},{1,5},{3,7},{5,9},{7,11},{... | collective-permute-start | bytes 786440 | tf_op jit(solution)/shard_map/ppermute | solution.py:234
  6.0 1.3 %collective-permute-start.3 = (bf16[16,8192]{1,0:T(8,128)(2,1)S(1)}, bf16[16,8192]{1,0:T(8,128)(2,1)S(1)}, u32[]{:S(2)}, u32[]{:S(2)}) collective-permute-start(bf16[16,8192]{1,0:T(8,128)(2,1)S(1)} %reshape.8.refs_0_), channel_id=1, source_target_pairs={{4,0},{6,2},{8,4},{10,6},{12,8},{14,10},{5,1},{7,3},{9,5},{11,7},{... | collective-permute-start | bytes 786440 | tf_op jit(solution)/shard_map/ppermute | solution.py:234
  7.3 4.2 %collective-permute-done.1.refs_2_ = bf16[16,8192]{1,0:T(8,128)(2,1)S(1)} collective-permute-done((bf16[16,8192]{1,0:T(8,128)(2,1)S(1)}, bf16[16,8192]{1,0:T(8,128)(2,1)S(1)}, u32[]{:S(2)}, u32[]{:S(2)}) %collective-permute-start.1) | collective-permute-done | bytes 262176 | tf_op jit(solution)/shard_map/ppermute | solution.py:234
  11.6 0.7 collective-permute-start.2
  12.2 3.5 %collective-permute-done.3.refs_11_ = bf16[16,8192]{1,0:T(8,128)(2,1)S(1)} collective-permute-done((bf16[16,8192]{1,0:T(8,128)(2,1)S(1)}, bf16[16,8192]{1,0:T(8,128)(2,1)S(1)}, u32[]{:S(2)}, u32[]{:S(2)}) %collective-permute-start.3) | collective-permute-done | bytes 262176 | tf_op jit(solution)/shard_map/ppermute | solution.py:234
  15.7 1.3 %collective-permute-start.4 = (bf16[16,8192]{1,0:T(8,128)(2,1)S(1)}, bf16[16,8192]{1,0:T(8,128)(2,1)S(1)}, u32[]{:S(2)}, u32[]{:S(2)}) collective-permute-start(bf16[16,8192]{1,0:T(8,128)(2,1)S(1)} %collective-permute-done.3.refs_11_), channel_id=1, source_target_pairs={{4,0},{6,2},{8,4},{10,6},{5,1},{7,3},{9,5},{11,7},{20,16},{22,18},... | collective-permute-start | bytes 786440 | tf_op jit(solution)/shard_map/ppermute | solution.py:234
  17.0 0.0 collective-permute-done.2.refs_6_
  17.0 7.6 %collective-permute-done.4.refs_7_ = bf16[16,8192]{1,0:T(8,128)(2,1)S(1)} collective-permute-done((bf16[16,8192]{1,0:T(8,128)(2,1)S(1)}, bf16[16,8192]{1,0:T(8,128)(2,1)S(1)}, u32[]{:S(2)}, u32[]{:S(2)}) %collective-permute-start.4) | collective-permute-done | bytes 262176 | tf_op jit(solution)/shard_map/ppermute | solution.py:234
  24.6 0.7 broadcast_select_fusion
  25.4 1.3 %collective-permute-start.5 = (bf16[16,8192]{1,0:T(8,128)(2,1)}, bf16[16,8192]{1,0:T(8,128)(2,1)S(1)}, u32[]{:S(2)}, u32[]{:S(2)}) collective-permute-start(bf16[16,8192]{1,0:T(8,128)(2,1)} %broadcast_select_fusion), channel_id=1, source_target_pairs={{4,0},{6,2},{8,12},{10,14},{5,1},{7,3},{9,13},{11,15},{20,16},{22,... | collective-permute-start | bytes 786440 | tf_op jit(solution)/shard_map/ppermute | solution.py:253
  26.6 7.2 %collective-permute-done.5.refs_3_.refs_10_ = bf16[16,8192]{1,0:T(8,128)(2,1)S(1)} collective-permute-done((bf16[16,8192]{1,0:T(8,128)(2,1)}, bf16[16,8192]{1,0:T(8,128)(2,1)S(1)}, u32[]{:S(2)}, u32[]{:S(2)}) %collective-permute-start.5) | collective-permute-done | bytes 262176 | tf_op jit(solution)/shard_map/ppermute | solution.py:253
  33.8 3.5 %all-to-all-start = ((bf16[8,128,256]{2,1,0:T(8,128)(2,1)}), bf16[8,128,256]{2,1,0:T(8,128)(2,1)S(1)}, u32[]{:S(2)}, u32[]{:S(2)}) async-start(bf16[8,128,256]{2,1,0:T(8,128)(2,1)} %param.15), calls=%async_computation | async-start | bytes 1048576 | tf_op jit(solution)/shard_map/all_to_all | solution.py:357
  37.3 1.9 %collective-permute-start = (bf16[16,8192]{1,0:T(8,128)(2,1)S(1)}, bf16[16,8192]{1,0:T(8,128)(2,1)S(1)}, u32[]{:S(2)}, u32[]{:S(2)}) collective-permute-start(bf16[16,8192]{1,0:T(8,128)(2,1)S(1)} %reshape.8.refs_0_), channel_id=1, source_target_pairs={{0,2},{2,0},{4,6},{6,4},{8,10},{10,8},{12,14},{14,12},{1,3},{3,1},... | collective-permute-start | bytes 786440 | tf_op jit(solution)/shard_map/ppermute | solution.py:239
  39.2 0.7 collective-permute-start.6
  39.9 2.1 %collective-permute-start.9 = (bf16[16,8192]{1,0:T(8,128)(2,1)S(1)}, bf16[16,8192]{1,0:T(8,128)(2,1)S(1)}, u32[]{:S(2)}, u32[]{:S(2)}) collective-permute-start(bf16[16,8192]{1,0:T(8,128)(2,1)S(1)} %collective-permute-done.3.refs_11_), channel_id=1, source_target_pairs={{0,2},{2,0},{4,6},{6,4},{8,10},{10,8},{1,3},{3,1},{5,7},{7,5},{9,1... | collective-permute-start | bytes 786440 | tf_op jit(solution)/shard_map/ppermute | solution.py:239
  42.0 1.9 %collective-permute-start.8 = (bf16[16,8192]{1,0:T(8,128)(2,1)}, bf16[16,8192]{1,0:T(8,128)(2,1)S(1)}, u32[]{:S(2)}, u32[]{:S(2)}) collective-permute-start(bf16[16,8192]{1,0:T(8,128)(2,1)} %broadcast_select_fusion), channel_id=1, source_target_pairs={{0,2},{2,0},{4,6},{6,4},{8,10},{10,8},{12,14},{14,12},{1,3},{3,1},... | collective-permute-start | bytes 786440 | tf_op jit(solution)/shard_map/ppermute | solution.py:254
  43.9 2.1 %collective-permute-start.7 = (bf16[16,8192]{1,0:T(8,128)(2,1)S(1)}, bf16[16,8192]{1,0:T(8,128)(2,1)S(1)}, u32[]{:S(2)}, u32[]{:S(2)}) collective-permute-start(bf16[16,8192]{1,0:T(8,128)(2,1)S(1)} %collective-permute-done.5.refs_3_.refs_10_), channel_id=1, source_target_pairs={{0,2},{2,0},{12,14},{14,12},{1,3},{3,1},{13,15},{15,13},{16,18},{1... | collective-permute-start | bytes 786440 | tf_op jit(solution)/shard_map/ppermute | solution.py:257
  46.1 0.1 stack.54.choice_ref
  46.2 0.1 stack.50.owner_ref
  46.3 0.0 copy-start.1
  46.3 4.6 %collective-permute-done.refs_1_ = bf16[16,8192]{1,0:T(8,128)(2,1)S(1)} collective-permute-done((bf16[16,8192]{1,0:T(8,128)(2,1)S(1)}, bf16[16,8192]{1,0:T(8,128)(2,1)S(1)}, u32[]{:S(2)}, u32[]{:S(2)}) %collective-permute-start) | collective-permute-done | bytes 262176 | tf_op jit(solution)/shard_map/ppermute | solution.py:239
  50.8 0.0 collective-permute-done.6.refs_4_
  50.8 5.6 %collective-permute-done.9.refs_13_ = bf16[16,8192]{1,0:T(8,128)(2,1)S(1)} collective-permute-done((bf16[16,8192]{1,0:T(8,128)(2,1)S(1)}, bf16[16,8192]{1,0:T(8,128)(2,1)S(1)}, u32[]{:S(2)}, u32[]{:S(2)}) %collective-permute-start.9) | collective-permute-done | bytes 262176 | tf_op jit(solution)/shard_map/ppermute | solution.py:239
  56.4 5.6 %collective-permute-done.8.refs_8_.refs_9_ = bf16[16,8192]{1,0:T(8,128)(2,1)S(1)} collective-permute-done((bf16[16,8192]{1,0:T(8,128)(2,1)}, bf16[16,8192]{1,0:T(8,128)(2,1)S(1)}, u32[]{:S(2)}, u32[]{:S(2)}) %collective-permute-start.8) | collective-permute-done | bytes 262176 | tf_op jit(solution)/shard_map/ppermute | solution.py:254
  62.0 2.9 %collective-permute-done.7.refs_5_.refs_12_ = bf16[16,8192]{1,0:T(8,128)(2,1)S(1)} collective-permute-done((bf16[16,8192]{1,0:T(8,128)(2,1)S(1)}, bf16[16,8192]{1,0:T(8,128)(2,1)S(1)}, u32[]{:S(2)}, u32[]{:S(2)}) %collective-permute-start.7) | collective-permute-done | bytes 262176 | tf_op jit(solution)/shard_map/ppermute | solution.py:257
  64.9 10.4 %project.1.token_ref = bf16[8,16,1280]{2,1,0:T(8,128)(2,1)} custom-call(s32[8]{0:T(128)S(1)} %stack.50.owner_ref, s32[8]{0:T(128)S(1)} %stack.54.choice_ref, bf16[16,8192]{1,0:T(8,128)(2,1)S(1)} %reshape.8.refs_0_, bf16[16,8192]{1,0:T(8,128)(2,1)S(1)} %collective-permute-done.refs_1_, bf16[16,8192]{1,0:T(8,128)(2,1)S(1)} %collective-permute-done.1.refs_2_, ...), custom_call_target="tpu_custom_call" | custom-call | flops 2684354560 | bytes 23068672 | tf_op jit(solution)/shard_map/project/pallas_call | solution.py:331
  75.3 0.0 copy-start
  75.3 0.0 all-to-all-done.prompt_ref
  75.4 4.6 %all-to-all-start.1 = ((bf16[8,16,1280]{2,1,0:T(8,128)(2,1)}), bf16[8,16,1280]{2,1,0:T(8,128)(2,1)S(1)}, u32[]{:S(2)}, u32[]{:S(2)}) async-start(bf16[8,16,1280]{2,1,0:T(8,128)(2,1)} %project.1.token_ref), calls=%async_computation.1 | async-start | bytes 655360 | tf_op jit(solution)/shard_map/all_to_all | solution.py:360
  79.9 0.0 copy-done.1
  80.0 0.1 copy.10
  80.0 0.1 reshape.7.table_ref
  80.8 2.1 %early.1.early_ref = bf16[2,256,2048]{2,1,0:T(8,128)(2,1)S(1)} custom-call(s32[16]{0:T(128)S(1)} %reshape.7.table_ref, bf16[8,16,1280]{2,1,0:T(8,128)(2,1)} %project.1.token_ref, bf16[16,128,2048]{2,1,0:T(8,128)(2,1)} %pool_ref.3), custom_call_target="tpu_custom_call" | custom-call | bytes 4194304 | tf_op jit(solution)/shard_map/early/pallas_call | solution.py:216
  82.9 5.7 %all-to-all-done.1.q_ref.kv_ref = bf16[8,16,1280]{2,1,0:T(8,128)(2,1)S(1)} async-done(((bf16[8,16,1280]{2,1,0:T(8,128)(2,1)}), bf16[8,16,1280]{2,1,0:T(8,128)(2,1)S(1)}, u32[]{:S(2)}, u32[]{:S(2)}) %all-to-all-start.1) | async-done | bytes 327712 | tf_op jit(solution)/shard_map/all_to_all | solution.py:360
  88.6 0.0 copy-done
  88.6 6.4 %attend.1 = bf16[8,2,8192]{2,1,0:T(2,128)(2,1)} custom-call(s32[16]{0:T(128)S(1)} %reshape.7.table_ref, s32[8]{0:T(128)S(1)} %copy-done, s32[1]{0:T(128)S(6)} %copy.11.slot_ref, bf16[8,16,1280]{2,1,0:T(8,128)(2,1)S(1)} %all-to-all-done.1.q_ref.kv_ref, bf16[8,16,1280]{2,1,0:T(8,128)(2,1)S(1)} %all-to-all-done.1.q_ref.kv_ref, ...), custom_call_target="tpu_custom_call" | custom-call | tf_op jit(solution)/shard_map/attend/pallas_call | solution.py:178
  (1 shorter events, 0.0 us)
Async XLA Ops:
  1.1 10.5 %collective-permute-start.1 = (bf16[16,8192]{1,0:T(8,128)(2,1)S(1)}, bf16[16,8192]{1,0:T(8,128)(2,1)S(1)}, u32[]{:S(2)}, u32[]{:S(2)}) collective-permute-start(bf16[16,8192]{1,0:T(8,128)(2,1)S(1)} %reshape.8.refs_0_), channel_id=1, source_target_pairs={{0,4},{2,6},{4,8},{6,10},{8,12},{10,14},{1,5},{3,7},{5,9},{7,11},{... | collective-permute-start | bytes 786440 | tf_op jit(solution)/shard_map/ppermute | solution.py:234
  6.0 9.7 %collective-permute-start.3 = (bf16[16,8192]{1,0:T(8,128)(2,1)S(1)}, bf16[16,8192]{1,0:T(8,128)(2,1)S(1)}, u32[]{:S(2)}, u32[]{:S(2)}) collective-permute-start(bf16[16,8192]{1,0:T(8,128)(2,1)S(1)} %reshape.8.refs_0_), channel_id=1, source_target_pairs={{4,0},{6,2},{8,4},{10,6},{12,8},{14,10},{5,1},{7,3},{9,5},{11,7},{... | collective-permute-start | bytes 786440 | tf_op jit(solution)/shard_map/ppermute | solution.py:234
  11.6 5.4 %collective-permute-start.2 = (bf16[16,8192]{1,0:T(8,128)(2,1)S(1)}, bf16[16,8192]{1,0:T(8,128)(2,1)S(1)}, u32[]{:S(2)}, u32[]{:S(2)}) collective-permute-start(bf16[16,8192]{1,0:T(8,128)(2,1)S(1)} %collective-permute-done.1.refs_2_), channel_id=1, source_target_pairs={{4,8},{6,10},{8,12},{10,14},{5,9},{7,11},{9,13},{11,15},{20,24},{2... | collective-permute-start | bytes 786440 | tf_op jit(solution)/shard_map/ppermute | solution.py:234
  15.7 8.9 %collective-permute-start.4 = (bf16[16,8192]{1,0:T(8,128)(2,1)S(1)}, bf16[16,8192]{1,0:T(8,128)(2,1)S(1)}, u32[]{:S(2)}, u32[]{:S(2)}) collective-permute-start(bf16[16,8192]{1,0:T(8,128)(2,1)S(1)} %collective-permute-done.3.refs_11_), channel_id=1, source_target_pairs={{4,0},{6,2},{8,4},{10,6},{5,1},{7,3},{9,5},{11,7},{20,16},{22,18},... | collective-permute-start | bytes 786440 | tf_op jit(solution)/shard_map/ppermute | solution.py:234
  25.4 8.5 %collective-permute-start.5 = (bf16[16,8192]{1,0:T(8,128)(2,1)}, bf16[16,8192]{1,0:T(8,128)(2,1)S(1)}, u32[]{:S(2)}, u32[]{:S(2)}) collective-permute-start(bf16[16,8192]{1,0:T(8,128)(2,1)} %broadcast_select_fusion), channel_id=1, source_target_pairs={{4,0},{6,2},{8,12},{10,14},{5,1},{7,3},{9,13},{11,15},{20,16},{22,... | collective-permute-start | bytes 786440 | tf_op jit(solution)/shard_map/ppermute | solution.py:253
  33.8 41.5 %all-to-all-start = ((bf16[8,128,256]{2,1,0:T(8,128)(2,1)}), bf16[8,128,256]{2,1,0:T(8,128)(2,1)S(1)}, u32[]{:S(2)}, u32[]{:S(2)}) async-start(bf16[8,128,256]{2,1,0:T(8,128)(2,1)} %param.15), calls=%async_computation | async-start | bytes 1048576 | tf_op jit(solution)/shard_map/all_to_all | solution.py:357
  37.3 13.5 %collective-permute-start = (bf16[16,8192]{1,0:T(8,128)(2,1)S(1)}, bf16[16,8192]{1,0:T(8,128)(2,1)S(1)}, u32[]{:S(2)}, u32[]{:S(2)}) collective-permute-start(bf16[16,8192]{1,0:T(8,128)(2,1)S(1)} %reshape.8.refs_0_), channel_id=1, source_target_pairs={{0,2},{2,0},{4,6},{6,4},{8,10},{10,8},{12,14},{14,12},{1,3},{3,1},... | collective-permute-start | bytes 786440 | tf_op jit(solution)/shard_map/ppermute | solution.py:239
  39.2 11.6 %collective-permute-start.6 = (bf16[16,8192]{1,0:T(8,128)(2,1)S(1)}, bf16[16,8192]{1,0:T(8,128)(2,1)S(1)}, u32[]{:S(2)}, u32[]{:S(2)}) collective-permute-start(bf16[16,8192]{1,0:T(8,128)(2,1)S(1)} %collective-permute-done.1.refs_2_), channel_id=1, source_target_pairs={{4,6},{6,4},{8,10},{10,8},{12,14},{14,12},{5,7},{7,5},{9,11},{11,9... | collective-permute-start | bytes 786440 | tf_op jit(solution)/shard_map/ppermute | solution.py:239
  39.9 16.5 %collective-permute-start.9 = (bf16[16,8192]{1,0:T(8,128)(2,1)S(1)}, bf16[16,8192]{1,0:T(8,128)(2,1)S(1)}, u32[]{:S(2)}, u32[]{:S(2)}) collective-permute-start(bf16[16,8192]{1,0:T(8,128)(2,1)S(1)} %collective-permute-done.3.refs_11_), channel_id=1, source_target_pairs={{0,2},{2,0},{4,6},{6,4},{8,10},{10,8},{1,3},{3,1},{5,7},{7,5},{9,1... | collective-permute-start | bytes 786440 | tf_op jit(solution)/shard_map/ppermute | solution.py:239
  42.0 20.0 %collective-permute-start.8 = (bf16[16,8192]{1,0:T(8,128)(2,1)}, bf16[16,8192]{1,0:T(8,128)(2,1)S(1)}, u32[]{:S(2)}, u32[]{:S(2)}) collective-permute-start(bf16[16,8192]{1,0:T(8,128)(2,1)} %broadcast_select_fusion), channel_id=1, source_target_pairs={{0,2},{2,0},{4,6},{6,4},{8,10},{10,8},{12,14},{14,12},{1,3},{3,1},... | collective-permute-start | bytes 786440 | tf_op jit(solution)/shard_map/ppermute | solution.py:254
  43.9 21.0 %collective-permute-start.7 = (bf16[16,8192]{1,0:T(8,128)(2,1)S(1)}, bf16[16,8192]{1,0:T(8,128)(2,1)S(1)}, u32[]{:S(2)}, u32[]{:S(2)}) collective-permute-start(bf16[16,8192]{1,0:T(8,128)(2,1)S(1)} %collective-permute-done.5.refs_3_.refs_10_), channel_id=1, source_target_pairs={{0,2},{2,0},{12,14},{14,12},{1,3},{3,1},{13,15},{15,13},{16,18},{1... | collective-permute-start | bytes 786440 | tf_op jit(solution)/shard_map/ppermute | solution.py:257
  46.3 33.7 %copy-start.1 = (s32[8,2]{0,1:T(2,128)S(1)}, s32[8,2]{0,1:T(2,128)}, u32[]{:S(2)}) copy-start(s32[8,2]{0,1:T(2,128)} %param.12) | copy-start | bytes 196
  75.3 13.3 %copy-start = (s32[8]{0:T(128)S(1)}, s32[8]{0:T(128)}, u32[]{:S(2)}) copy-start(s32[8]{0:T(128)} %lens_ref.1) | copy-start | bytes 100
  75.4 13.3 %all-to-all-start.1 = ((bf16[8,16,1280]{2,1,0:T(8,128)(2,1)}), bf16[8,16,1280]{2,1,0:T(8,128)(2,1)S(1)}, u32[]{:S(2)}, u32[]{:S(2)}) async-start(bf16[8,16,1280]{2,1,0:T(8,128)(2,1)} %project.1.token_ref), calls=%async_computation.1 | async-start | bytes 655360 | tf_op jit(solution)/shard_map/all_to_all | solution.py:360

commit v3 on v2

--- a/solution.py
+++ b/solution.py
@@ -16,6 +16,7 @@
 MASKED = -1e30
 PROJECT_LIMIT = 48 << 20
 AHEAD = 2
+LANES = 512
 PAGES_AHEAD = 3
 EARLY = 2
 EARLY_LIMIT = 50 << 20
@@ -91,12 +92,27 @@
 
     where_key = lax.broadcasted_iota(jnp.int32, (all_rows, span), 1)
 
-    def one_sequence(s, context):
-        at = pl.multiple_of(s * rows, rows)
+    def context_of(s):
+        if s < early:
+            return early_ref.at[s]
+        return pages.at[s - early]
+
+    def cached_scores(s):
+        if s >= early:
+            if s + PAGES_AHEAD < seqs:
+                for p in range(span_pages):
+                    page_copy(s + PAGES_AHEAD, p).start()
+            for p in range(span_pages):
+                page_copy(s, p).wait()
+        context = context_of(s)
         sc = jnp.concatenate(
             [scaled(q_pairs[j, s], context[:, j * wide : (j + 1) * wide]) for j in range(pairs)]
         )
-        sc = jnp.where(where_key < lens_ref[s], sc, MASKED)
+        return jnp.where(where_key < lens_ref[s], sc, MASKED)
+
+    def one_sequence(s, sc):
+        part_rows = slice(s * rows, (s + 1) * rows)
+        context = context_of(s)
         sn = new_scores[s]
         top = jnp.maximum(jnp.max(sc, axis=1, keepdims=True), jnp.max(sn, axis=1, keepdims=True))
         ec = jnp.exp(sc - top)
@@ -106,27 +122,18 @@
         for j in range(pairs):
             col = value_at + j * wide
             both = mix(ec[j * 2 * rows : (j + 1) * 2 * rows], context[:, col : col + wide])
-            acc[2 * j, pl.ds(at, rows), :] = both[:rows, :HEAD_SIZE]
-            acc[2 * j + 1, pl.ds(at, rows), :] = both[rows:, HEAD_SIZE:]
+            acc[2 * j, part_rows, :] = both[:rows, :HEAD_SIZE]
+            acc[2 * j + 1, part_rows, :] = both[rows:, HEAD_SIZE:]
         for k in heads:
             part = slice(k * rows, (k + 1) * rows)
-            top_all[k, pl.ds(at, rows), :] = jnp.broadcast_to(top[part], (rows, HEAD_SIZE))
-            sum_all[k, pl.ds(at, rows), :] = jnp.broadcast_to(total[part], (rows, HEAD_SIZE))
-
-    @pl.loop(0, early)
-    def _(s):
-        one_sequence(s, early_ref.at[s])
-
-    @pl.loop(early, seqs)
-    def _(s):
-        @pl.when(s + PAGES_AHEAD < seqs)
-        def _():
-            for p in range(span_pages):
-                page_copy(s + PAGES_AHEAD, p).start()
-
-        for p in range(span_pages):
-            page_copy(s, p).wait()
-        one_sequence(s, pages.at[s - early])
+            top_all[k, part_rows, :] = jnp.broadcast_to(top[part], (rows, HEAD_SIZE))
+            sum_all[k, part_rows, :] = jnp.broadcast_to(total[part], (rows, HEAD_SIZE))
+
+    scores = cached_scores(0)
+    for s in range(seqs):
+        following = cached_scores(s + 1) if s + 1 < seqs else None
+        one_sequence(s, scores)
+        scores = following
 
     for j in range(pairs):
         w = new_weights[:, j * 2 * rows : (j + 1) * 2 * rows, :].reshape(seqs * 2 * rows, new_rows)
@@ -268,13 +275,13 @@
 def project_kernel(owner_ref, choice_ref, *refs, tiles, counts):
     blocks = sum(counts)
     sources = refs[:blocks]
-    wq_ref, wkv_ref, out_ref, x_here, w_here, x_sems, w_sems = refs[blocks:]
+    wq_ref, wkv_ref, out_ref, x_raw, x_here, w_here, x_sems, w_sems = refs[blocks:]
     size, tokens, _ = out_ref.shape
+    seqs = sources[0].shape[0]
     q_width = wq_ref.shape[1]
 
     def fetch(j, source):
-        rows = pl.ds(pl.multiple_of(owner_ref[j] * tokens, tokens), tokens)
-        return pltpu.make_async_copy(source, x_here.at[rows], x_sems.at[j])
+        return pltpu.make_async_copy(source, x_raw.at[pl.ds(owner_ref[j] * seqs, seqs)], x_sems.at[j])
 
     at = 0
     firsts = []
@@ -303,6 +310,11 @@
     for j, source in enumerate(firsts):
         fetch(j, source).wait()
 
+    @pl.loop(0, x_raw.shape[2] // LANES)
+    def _(c):
+        cols = pl.ds(pl.multiple_of(c * LANES, LANES), LANES)
+        x_here[:, cols] = x_raw[:, :, cols].reshape(size * tokens, LANES)
+
     for i, (at, width) in enumerate(tiles):
         copies[i].wait()
         if i + AHEAD < len(tiles):
@@ -315,7 +327,8 @@
 
 def project(found, wq, wkv):
     size = len(found)
-    tokens = found[0][0][0].shape[0]
+    block = found[0][0][0].shape
+    tokens = block[0] * block[1]
     depth, q_width = wq.shape
     width = q_width + wkv.shape[1]
     wide = 2 * HEAD_SIZE
@@ -334,6 +347,7 @@
         in_specs=[smem, smem] + [hbm] * len(sources) + [hbm, hbm],
         out_specs=vmem,
         scratch_shapes=[
+            pltpu.VMEM((size * block[0], block[1], depth), wq.dtype),
             pltpu.VMEM((size * tokens, depth), wq.dtype),
             pltpu.VMEM((depth, width), wq.dtype),
             pltpu.SemaphoreType.DMA((size,)),
@@ -346,13 +360,11 @@
             transcendentals=0,
         ),
         name="project",
-    )(owners, choices, *sources, wq, wkv)
+    )(owners, choices, pltpu.with_memory_space_constraint(sources[0], pltpu.HBM), *sources[1:], wq, wkv)
 
 
 def per_device(size, hidden, wq, wkv, cache_pool, page_table, ctx_len, prompt_slot, prompt_kv):
-    tokens = hidden.shape[0] * hidden.shape[1]
-    own = hidden.reshape(tokens, hidden.shape[2])
-    found, late = gather_blocks(own, "tensor", size)
+    found, late = gather_blocks(hidden, "tensor", size)
     prompt_kv, _ = lax.optimization_barrier((prompt_kv, late))
     prompt = lax.all_to_all(prompt_kv, "tensor", split_axis=0, concat_axis=0, tiled=True)
     joined = project(found, wq, wkv)

time: 95.5 us -> 93.2 us (0.976)
  local copies, waits for them, and re-layouts: 1.4 us -> 0.35 us
    reshape x1 -> x0, local copies, waits for them, and re-layouts: 1.05 us -> none  [per_device(): own = hidden.reshape(tokens, hidden.shape[2])]
where the time goes in v3:
time: 93.2 us; the launch traced here: 92.7 us
  waiting for transfers between devices  46.9 us (50%)
  starting transfers between devices  26.2 us (28%)
  Pallas kernels  18.4 us (20%)
    ppermute x4, waiting for transfers between devices, hop(): lax.ppermute(x, axis, [(2 * c + p, 2 * (c + step) + p) for c in range(fir...  15.5 us
    pallas_call x1, Pallas kernels, project(): pl.pallas_call(functools.partial(project_kernel, tiles=tiles, counts=coun...  10.4 us
    ppermute x3, waiting for transfers between devices, swap(): lax.ppermute(x, axis, [(2 * c + p, 2 * c + 1 - p) for c in range(first, l...  10.2 us
    ppermute x4, starting transfers between devices, hop(): lax.ppermute(x, axis, [(2 * c + p, 2 * (c + step) + p) for c in range(fir...  8.2 us
    ppermute x1, waiting for transfers between devices, gather_blocks(): lax.ppermute(both, axis, [(2 * a + p, 2 * b + p) for a, b in ends for p i...  6.97 us
    pallas_call x1, Pallas kernels, attend(): pl.pallas_call(kernel, out_shape=jax.ShapeDtypeStruct((seqs, STEPS, QUERY...  5.88 us
    all_to_all x1, waiting for transfers between devices, per_device(): lax.all_to_all(joined, 'tensor', split_axis=0, concat_axis=0, tiled=True)  5.74 us
    ppermute x1, waiting for transfers between devices, gather_blocks(): lax.ppermute(both, axis, [(2 * c + p, 2 * c + 1 - p) for c in (0, 1, line...  5.62 us
  transfers between devices with their start and end apart: 12, of which 9 were waited for; matrix products, arithmetic and copies ran while one was open for 0% of the time, Pallas kernels for 13%

profile of v3, /device:TPU:0, one launch (start us, length us, event | category | flops | bytes accessed | tf_op | source)
XLA Modules:
  0.0 92.7 jit_solution(11381601155135187060)
XLA Ops:
  0.0 5.0 %collective-permute-start.1 = (bf16[8,2,8192]{2,1,0:T(2,128)(2,1)}, bf16[8,2,8192]{2,1,0:T(2,128)(2,1)S(1)}, u32[]{:S(2)}, u32[]{:S(2)}) collective-permute-start(bf16[8,2,8192]{2,1,0:T(2,128)(2,1)} %refs_0_.1), channel_id=1, source_target_pairs={{0,4},{2,6},{4,8},{6,10},{8,12},{10,14},{1,5},{3,7},{5,9},{7,11},{... | collective-permute-start | bytes 786440 | tf_op jit(solution)/shard_map/ppermute | solution.py:241
  5.0 1.3 %collective-permute-start.3 = (bf16[8,2,8192]{2,1,0:T(2,128)(2,1)}, bf16[8,2,8192]{2,1,0:T(2,128)(2,1)S(1)}, u32[]{:S(2)}, u32[]{:S(2)}) collective-permute-start(bf16[8,2,8192]{2,1,0:T(2,128)(2,1)} %refs_0_.1), channel_id=1, source_target_pairs={{4,0},{6,2},{8,4},{10,6},{12,8},{14,10},{5,1},{7,3},{9,5},{11,7},{... | collective-permute-start | bytes 786440 | tf_op jit(solution)/shard_map/ppermute | solution.py:241
  6.3 4.5 %collective-permute-done.1.refs_2_ = bf16[8,2,8192]{2,1,0:T(2,128)(2,1)S(1)} collective-permute-done((bf16[8,2,8192]{2,1,0:T(2,128)(2,1)}, bf16[8,2,8192]{2,1,0:T(2,128)(2,1)S(1)}, u32[]{:S(2)}, u32[]{:S(2)}) %collective-permute-start.1) | collective-permute-done | bytes 262176 | tf_op jit(solution)/shard_map/ppermute | solution.py:241
  10.8 0.7 collective-permute-start.2
  11.5 3.4 %collective-permute-done.3.refs_11_ = bf16[8,2,8192]{2,1,0:T(2,128)(2,1)S(1)} collective-permute-done((bf16[8,2,8192]{2,1,0:T(2,128)(2,1)}, bf16[8,2,8192]{2,1,0:T(2,128)(2,1)S(1)}, u32[]{:S(2)}, u32[]{:S(2)}) %collective-permute-start.3) | collective-permute-done | bytes 262176 | tf_op jit(solution)/shard_map/ppermute | solution.py:241
  14.8 1.3 %collective-permute-start.4 = (bf16[8,2,8192]{2,1,0:T(2,128)(2,1)S(1)}, bf16[8,2,8192]{2,1,0:T(2,128)(2,1)S(1)}, u32[]{:S(2)}, u32[]{:S(2)}) collective-permute-start(bf16[8,2,8192]{2,1,0:T(2,128)(2,1)S(1)} %collective-permute-done.3.refs_11_), channel_id=1, source_target_pairs={{4,0},{6,2},{8,4},{10,6},{5,1},{7,3},{9,5},{11,7},{20,16},{22,18},... | collective-permute-start | bytes 786440 | tf_op jit(solution)/shard_map/ppermute | solution.py:241
  16.1 0.0 collective-permute-done.2.refs_6_
  16.2 7.6 %collective-permute-done.4.refs_7_ = bf16[8,2,8192]{2,1,0:T(2,128)(2,1)S(1)} collective-permute-done((bf16[8,2,8192]{2,1,0:T(2,128)(2,1)S(1)}, bf16[8,2,8192]{2,1,0:T(2,128)(2,1)S(1)}, u32[]{:S(2)}, u32[]{:S(2)}) %collective-permute-start.4) | collective-permute-done | bytes 262176 | tf_op jit(solution)/shard_map/ppermute | solution.py:241
  23.8 1.3 %collective-permute-start.5 = (bf16[8,2,8192]{2,1,0:T(2,128)(2,1)S(1)}, bf16[8,2,8192]{2,1,0:T(2,128)(2,1)S(1)}, u32[]{:S(2)}, u32[]{:S(2)}) collective-permute-start(bf16[8,2,8192]{2,1,0:T(2,128)(2,1)S(1)} %bitcast.16), channel_id=1, source_target_pairs={{4,0},{6,2},{8,12},{10,14},{5,1},{7,3},{9,13},{11,15},{20,16},{22,... | collective-permute-start | bytes 786440 | tf_op jit(solution)/shard_map/ppermute | solution.py:260
  25.1 7.0 %collective-permute-done.5.refs_3_.refs_10_ = bf16[8,2,8192]{2,1,0:T(2,128)(2,1)S(1)} collective-permute-done((bf16[8,2,8192]{2,1,0:T(2,128)(2,1)S(1)}, bf16[8,2,8192]{2,1,0:T(2,128)(2,1)S(1)}, u32[]{:S(2)}, u32[]{:S(2)}) %collective-permute-start.5) | collective-permute-done | bytes 262176 | tf_op jit(solution)/shard_map/ppermute | solution.py:260
  32.1 3.5 %all-to-all-start = ((bf16[8,128,256]{2,1,0:T(8,128)(2,1)}), bf16[8,128,256]{2,1,0:T(8,128)(2,1)S(1)}, u32[]{:S(2)}, u32[]{:S(2)}) async-start(bf16[8,128,256]{2,1,0:T(8,128)(2,1)} %param.15), calls=%async_computation | async-start | bytes 1048576 | tf_op jit(solution)/shard_map/all_to_all | solution.py:369
  35.6 1.9 %collective-permute-start = (bf16[8,2,8192]{2,1,0:T(2,128)(2,1)}, bf16[8,2,8192]{2,1,0:T(2,128)(2,1)S(1)}, u32[]{:S(2)}, u32[]{:S(2)}) collective-permute-start(bf16[8,2,8192]{2,1,0:T(2,128)(2,1)} %refs_0_.1), channel_id=1, source_target_pairs={{0,2},{2,0},{4,6},{6,4},{8,10},{10,8},{12,14},{14,12},{1,3},{3,1},... | collective-permute-start | bytes 786440 | tf_op jit(solution)/shard_map/ppermute | solution.py:246
  37.5 0.7 collective-permute-start.6
  38.2 2.1 %collective-permute-start.9 = (bf16[8,2,8192]{2,1,0:T(2,128)(2,1)S(1)}, bf16[8,2,8192]{2,1,0:T(2,128)(2,1)S(1)}, u32[]{:S(2)}, u32[]{:S(2)}) collective-permute-start(bf16[8,2,8192]{2,1,0:T(2,128)(2,1)S(1)} %collective-permute-done.3.refs_11_), channel_id=1, source_target_pairs={{0,2},{2,0},{4,6},{6,4},{8,10},{10,8},{1,3},{3,1},{5,7},{7,5},{9,1... | collective-permute-start | bytes 786440 | tf_op jit(solution)/shard_map/ppermute | solution.py:246
  40.3 1.9 %collective-permute-start.8 = (bf16[8,2,8192]{2,1,0:T(2,128)(2,1)S(1)}, bf16[8,2,8192]{2,1,0:T(2,128)(2,1)S(1)}, u32[]{:S(2)}, u32[]{:S(2)}) collective-permute-start(bf16[8,2,8192]{2,1,0:T(2,128)(2,1)S(1)} %bitcast.17), channel_id=1, source_target_pairs={{0,2},{2,0},{4,6},{6,4},{8,10},{10,8},{12,14},{14,12},{1,3},{3,1},... | collective-permute-start | bytes 786440 | tf_op jit(solution)/shard_map/ppermute | solution.py:261
  42.2 2.1 %collective-permute-start.7 = (bf16[8,2,8192]{2,1,0:T(2,128)(2,1)S(1)}, bf16[8,2,8192]{2,1,0:T(2,128)(2,1)S(1)}, u32[]{:S(2)}, u32[]{:S(2)}) collective-permute-start(bf16[8,2,8192]{2,1,0:T(2,128)(2,1)S(1)} %collective-permute-done.5.refs_3_.refs_10_), channel_id=1, source_target_pairs={{0,2},{2,0},{12,14},{14,12},{1,3},{3,1},{13,15},{15,13},{16,18},{1... | collective-permute-start | bytes 786440 | tf_op jit(solution)/shard_map/ppermute | solution.py:264
  44.3 0.1 stack.54.choice_ref
  44.4 0.1 stack.50.owner_ref
  44.5 0.0 copy-start.1
  44.5 4.5 %collective-permute-done.refs_1_ = bf16[8,2,8192]{2,1,0:T(2,128)(2,1)S(1)} collective-permute-done((bf16[8,2,8192]{2,1,0:T(2,128)(2,1)}, bf16[8,2,8192]{2,1,0:T(2,128)(2,1)S(1)}, u32[]{:S(2)}, u32[]{:S(2)}) %collective-permute-start) | collective-permute-done | bytes 262176 | tf_op jit(solution)/shard_map/ppermute | solution.py:246
  49.1 0.0 collective-permute-done.6.refs_4_
  49.1 5.6 %collective-permute-done.9.refs_13_ = bf16[8,2,8192]{2,1,0:T(2,128)(2,1)S(1)} collective-permute-done((bf16[8,2,8192]{2,1,0:T(2,128)(2,1)S(1)}, bf16[8,2,8192]{2,1,0:T(2,128)(2,1)S(1)}, u32[]{:S(2)}, u32[]{:S(2)}) %collective-permute-start.9) | collective-permute-done | bytes 262176 | tf_op jit(solution)/shard_map/ppermute | solution.py:246
  54.7 5.6 %collective-permute-done.8.refs_8_.refs_9_ = bf16[8,2,8192]{2,1,0:T(2,128)(2,1)S(1)} collective-permute-done((bf16[8,2,8192]{2,1,0:T(2,128)(2,1)S(1)}, bf16[8,2,8192]{2,1,0:T(2,128)(2,1)S(1)}, u32[]{:S(2)}, u32[]{:S(2)}) %collective-permute-start.8) | collective-permute-done | bytes 262176 | tf_op jit(solution)/shard_map/ppermute | solution.py:261
  60.3 2.9 %collective-permute-done.7.refs_5_.refs_12_ = bf16[8,2,8192]{2,1,0:T(2,128)(2,1)S(1)} collective-permute-done((bf16[8,2,8192]{2,1,0:T(2,128)(2,1)S(1)}, bf16[8,2,8192]{2,1,0:T(2,128)(2,1)S(1)}, u32[]{:S(2)}, u32[]{:S(2)}) %collective-permute-start.7) | collective-permute-done | bytes 262176 | tf_op jit(solution)/shard_map/ppermute | solution.py:264
  63.2 10.4 %project.1.token_ref = bf16[8,16,1280]{2,1,0:T(8,128)(2,1)} custom-call(s32[8]{0:T(128)S(1)} %stack.50.owner_ref, s32[8]{0:T(128)S(1)} %stack.54.choice_ref, bf16[8,2,8192]{2,1,0:T(2,128)(2,1)} %refs_0_.1, bf16[8,2,8192]{2,1,0:T(2,128)(2,1)S(1)} %collective-permute-done.refs_1_, bf16[8,2,8192]{2,1,0:T(2,128)(2,1)S(1)} %collective-permute-done.1.refs_2_, ...), custom_call_target="tpu_custom_call" | custom-call | flops 2684354560 | bytes 23068672 | tf_op jit(solution)/shard_map/project/pallas_call | solution.py:344
  73.6 0.0 copy-start
  73.6 0.0 all-to-all-done.prompt_ref
  73.6 4.6 %all-to-all-start.1 = ((bf16[8,16,1280]{2,1,0:T(8,128)(2,1)}), bf16[8,16,1280]{2,1,0:T(8,128)(2,1)S(1)}, u32[]{:S(2)}, u32[]{:S(2)}) async-start(bf16[8,16,1280]{2,1,0:T(8,128)(2,1)} %project.1.token_ref), calls=%async_computation.1 | async-start | bytes 655360 | tf_op jit(solution)/shard_map/all_to_all | solution.py:372
  78.2 0.0 copy-done.1
  78.2 0.1 copy.10
  78.3 0.1 reshape.4.table_ref
  79.0 2.1 %early.1.early_ref = bf16[2,256,2048]{2,1,0:T(8,128)(2,1)S(1)} custom-call(s32[16]{0:T(128)S(1)} %reshape.4.table_ref, bf16[8,16,1280]{2,1,0:T(8,128)(2,1)} %project.1.token_ref, bf16[16,128,2048]{2,1,0:T(8,128)(2,1)} %pool_ref.3), custom_call_target="tpu_custom_call" | custom-call | bytes 4194304 | tf_op jit(solution)/shard_map/early/pallas_call | solution.py:223
  81.1 5.7 %all-to-all-done.1.q_ref.kv_ref = bf16[8,16,1280]{2,1,0:T(8,128)(2,1)S(1)} async-done(((bf16[8,16,1280]{2,1,0:T(8,128)(2,1)}), bf16[8,16,1280]{2,1,0:T(8,128)(2,1)S(1)}, u32[]{:S(2)}, u32[]{:S(2)}) %all-to-all-start.1) | async-done | bytes 327712 | tf_op jit(solution)/shard_map/all_to_all | solution.py:372
  86.8 0.0 copy-done
  86.8 5.9 %attend.1 = bf16[8,2,8192]{2,1,0:T(2,128)(2,1)} custom-call(s32[16]{0:T(128)S(1)} %reshape.4.table_ref, s32[8]{0:T(128)S(1)} %copy-done, s32[1]{0:T(128)S(6)} %copy.11.slot_ref, bf16[8,16,1280]{2,1,0:T(8,128)(2,1)S(1)} %all-to-all-done.1.q_ref.kv_ref, bf16[8,16,1280]{2,1,0:T(8,128)(2,1)S(1)} %all-to-all-done.1.q_ref.kv_ref, ...), custom_call_target="tpu_custom_call" | custom-call | tf_op jit(solution)/shard_map/attend/pallas_call | solution.py:185
  (2 shorter events, 0.0 us)
Async XLA Ops:
  0.0 10.8 %collective-permute-start.1 = (bf16[8,2,8192]{2,1,0:T(2,128)(2,1)}, bf16[8,2,8192]{2,1,0:T(2,128)(2,1)S(1)}, u32[]{:S(2)}, u32[]{:S(2)}) collective-permute-start(bf16[8,2,8192]{2,1,0:T(2,128)(2,1)} %refs_0_.1), channel_id=1, source_target_pairs={{0,4},{2,6},{4,8},{6,10},{8,12},{10,14},{1,5},{3,7},{5,9},{7,11},{... | collective-permute-start | bytes 786440 | tf_op jit(solution)/shard_map/ppermute | solution.py:241
  5.0 9.9 %collective-permute-start.3 = (bf16[8,2,8192]{2,1,0:T(2,128)(2,1)}, bf16[8,2,8192]{2,1,0:T(2,128)(2,1)S(1)}, u32[]{:S(2)}, u32[]{:S(2)}) collective-permute-start(bf16[8,2,8192]{2,1,0:T(2,128)(2,1)} %refs_0_.1), channel_id=1, source_target_pairs={{4,0},{6,2},{8,4},{10,6},{12,8},{14,10},{5,1},{7,3},{9,5},{11,7},{... | collective-permute-start | bytes 786440 | tf_op jit(solution)/shard_map/ppermute | solution.py:241
  10.8 5.3 %collective-permute-start.2 = (bf16[8,2,8192]{2,1,0:T(2,128)(2,1)S(1)}, bf16[8,2,8192]{2,1,0:T(2,128)(2,1)S(1)}, u32[]{:S(2)}, u32[]{:S(2)}) collective-permute-start(bf16[8,2,8192]{2,1,0:T(2,128)(2,1)S(1)} %collective-permute-done.1.refs_2_), channel_id=1, source_target_pairs={{4,8},{6,10},{8,12},{10,14},{5,9},{7,11},{9,13},{11,15},{20,24},{2... | collective-permute-start | bytes 786440 | tf_op jit(solution)/shard_map/ppermute | solution.py:241
  14.8 8.9 %collective-permute-start.4 = (bf16[8,2,8192]{2,1,0:T(2,128)(2,1)S(1)}, bf16[8,2,8192]{2,1,0:T(2,128)(2,1)S(1)}, u32[]{:S(2)}, u32[]{:S(2)}) collective-permute-start(bf16[8,2,8192]{2,1,0:T(2,128)(2,1)S(1)} %collective-permute-done.3.refs_11_), channel_id=1, source_target_pairs={{4,0},{6,2},{8,4},{10,6},{5,1},{7,3},{9,5},{11,7},{20,16},{22,18},... | collective-permute-start | bytes 786440 | tf_op jit(solution)/shard_map/ppermute | solution.py:241
  23.8 8.3 %collective-permute-start.5 = (bf16[8,2,8192]{2,1,0:T(2,128)(2,1)S(1)}, bf16[8,2,8192]{2,1,0:T(2,128)(2,1)S(1)}, u32[]{:S(2)}, u32[]{:S(2)}) collective-permute-start(bf16[8,2,8192]{2,1,0:T(2,128)(2,1)S(1)} %bitcast.16), channel_id=1, source_target_pairs={{4,0},{6,2},{8,12},{10,14},{5,1},{7,3},{9,13},{11,15},{20,16},{22,... | collective-permute-start | bytes 786440 | tf_op jit(solution)/shard_map/ppermute | solution.py:260
  32.1 41.5 %all-to-all-start = ((bf16[8,128,256]{2,1,0:T(8,128)(2,1)}), bf16[8,128,256]{2,1,0:T(8,128)(2,1)S(1)}, u32[]{:S(2)}, u32[]{:S(2)}) async-start(bf16[8,128,256]{2,1,0:T(8,128)(2,1)} %param.15), calls=%async_computation | async-start | bytes 1048576 | tf_op jit(solution)/shard_map/all_to_all | solution.py:369
  35.6 13.5 %collective-permute-start = (bf16[8,2,8192]{2,1,0:T(2,128)(2,1)}, bf16[8,2,8192]{2,1,0:T(2,128)(2,1)S(1)}, u32[]{:S(2)}, u32[]{:S(2)}) collective-permute-start(bf16[8,2,8192]{2,1,0:T(2,128)(2,1)} %refs_0_.1), channel_id=1, source_target_pairs={{0,2},{2,0},{4,6},{6,4},{8,10},{10,8},{12,14},{14,12},{1,3},{3,1},... | collective-permute-start | bytes 786440 | tf_op jit(solution)/shard_map/ppermute | solution.py:246
  37.5 11.6 %collective-permute-start.6 = (bf16[8,2,8192]{2,1,0:T(2,128)(2,1)S(1)}, bf16[8,2,8192]{2,1,0:T(2,128)(2,1)S(1)}, u32[]{:S(2)}, u32[]{:S(2)}) collective-permute-start(bf16[8,2,8192]{2,1,0:T(2,128)(2,1)S(1)} %collective-permute-done.1.refs_2_), channel_id=1, source_target_pairs={{4,6},{6,4},{8,10},{10,8},{12,14},{14,12},{5,7},{7,5},{9,11},{11,9... | collective-permute-start | bytes 786440 | tf_op jit(solution)/shard_map/ppermute | solution.py:246
  38.2 16.5 %collective-permute-start.9 = (bf16[8,2,8192]{2,1,0:T(2,128)(2,1)S(1)}, bf16[8,2,8192]{2,1,0:T(2,128)(2,1)S(1)}, u32[]{:S(2)}, u32[]{:S(2)}) collective-permute-start(bf16[8,2,8192]{2,1,0:T(2,128)(2,1)S(1)} %collective-permute-done.3.refs_11_), channel_id=1, source_target_pairs={{0,2},{2,0},{4,6},{6,4},{8,10},{10,8},{1,3},{3,1},{5,7},{7,5},{9,1... | collective-permute-start | bytes 786440 | tf_op jit(solution)/shard_map/ppermute | solution.py:246
  40.3 20.0 %collective-permute-start.8 = (bf16[8,2,8192]{2,1,0:T(2,128)(2,1)S(1)}, bf16[8,2,8192]{2,1,0:T(2,128)(2,1)S(1)}, u32[]{:S(2)}, u32[]{:S(2)}) collective-permute-start(bf16[8,2,8192]{2,1,0:T(2,128)(2,1)S(1)} %bitcast.17), channel_id=1, source_target_pairs={{0,2},{2,0},{4,6},{6,4},{8,10},{10,8},{12,14},{14,12},{1,3},{3,1},... | collective-permute-start | bytes 786440 | tf_op jit(solution)/shard_map/ppermute | solution.py:261
  42.2 21.0 %collective-permute-start.7 = (bf16[8,2,8192]{2,1,0:T(2,128)(2,1)S(1)}, bf16[8,2,8192]{2,1,0:T(2,128)(2,1)S(1)}, u32[]{:S(2)}, u32[]{:S(2)}) collective-permute-start(bf16[8,2,8192]{2,1,0:T(2,128)(2,1)S(1)} %collective-permute-done.5.refs_3_.refs_10_), channel_id=1, source_target_pairs={{0,2},{2,0},{12,14},{14,12},{1,3},{3,1},{13,15},{15,13},{16,18},{1... | collective-permute-start | bytes 786440 | tf_op jit(solution)/shard_map/ppermute | solution.py:264
  44.5 33.7 %copy-start.1 = (s32[8,2]{0,1:T(2,128)S(1)}, s32[8,2]{0,1:T(2,128)}, u32[]{:S(2)}) copy-start(s32[8,2]{0,1:T(2,128)} %param.12) | copy-start | bytes 196
  73.6 13.3 %copy-start = (s32[8]{0:T(128)S(1)}, s32[8]{0:T(128)}, u32[]{:S(2)}) copy-start(s32[8]{0:T(128)} %lens_ref.1) | copy-start | bytes 100
  73.6 13.3 %all-to-all-start.1 = ((bf16[8,16,1280]{2,1,0:T(8,128)(2,1)}), bf16[8,16,1280]{2,1,0:T(8,128)(2,1)S(1)}, u32[]{:S(2)}, u32[]{:S(2)}) async-start(bf16[8,16,1280]{2,1,0:T(8,128)(2,1)} %project.1.token_ref), calls=%async_computation.1 | async-start | bytes 655360 | tf_op jit(solution)/shard_map/all_to_all | solution.py:372

commit v4 on v3

--- a/solution.py
+++ b/solution.py
@@ -15,7 +15,7 @@
 STEPS = 2
 MASKED = -1e30
 PROJECT_LIMIT = 48 << 20
-AHEAD = 2
+AHEAD = 3
 LANES = 512
 PAGES_AHEAD = 3
 EARLY = 2
@@ -275,7 +275,7 @@
 def project_kernel(owner_ref, choice_ref, *refs, tiles, counts):
     blocks = sum(counts)
     sources = refs[:blocks]
-    wq_ref, wkv_ref, out_ref, x_raw, x_here, w_here, x_sems, w_sems = refs[blocks:]
+    wq_ref, wkv_ref, out_ref, x_raw, x_here, x_sems, w_sems, *w_here = refs[blocks:]
     size, tokens, _ = out_ref.shape
     seqs = sources[0].shape[0]
     q_width = wq_ref.shape[1]
@@ -304,7 +304,7 @@
     copies = []
     for i, (at, width) in enumerate(tiles):
         source = wq_ref.at[:, pl.ds(at, width)] if at < q_width else wkv_ref.at[:, pl.ds(at - q_width, width)]
-        copies.append(pltpu.make_async_copy(source, w_here.at[:, pl.ds(at, width)], w_sems.at[i]))
+        copies.append(pltpu.make_async_copy(source, w_here[i], w_sems.at[i]))
     for c in copies[:AHEAD]:
         c.start()
     for j, source in enumerate(firsts):
@@ -320,7 +320,7 @@
         if i + AHEAD < len(tiles):
             copies[i + AHEAD].start()
         cols = slice(at, at + width)
-        y = jnp.dot(x_here[...], w_here[:, cols], preferred_element_type=jnp.float32).astype(jnp.bfloat16)
+        y = jnp.dot(x_here[...], w_here[i][...], preferred_element_type=jnp.float32).astype(jnp.bfloat16)
         for j in range(size):
             out_ref[j, :, cols] = y[j * tokens : (j + 1) * tokens]
 
@@ -333,7 +333,7 @@
     width = q_width + wkv.shape[1]
     wide = 2 * HEAD_SIZE
     tiles = [(at, min(wide, q_width - at)) for at in range(0, q_width, wide)]
-    tiles += [(at, min(HEAD_SIZE, width - at)) for at in range(q_width, width, HEAD_SIZE)]
+    tiles += [(at, min(wide, width - at)) for at in range(q_width, width, wide)]
     counts = [len(options) for options, _, _ in found]
     sources = [block for options, _, _ in found for block in options]
     choices = jnp.stack([jnp.asarray(choice, jnp.int32) for _, choice, _ in found])
@@ -349,10 +349,10 @@
         scratch_shapes=[
             pltpu.VMEM((size * block[0], block[1], depth), wq.dtype),
             pltpu.VMEM((size * tokens, depth), wq.dtype),
-            pltpu.VMEM((depth, width), wq.dtype),
             pltpu.SemaphoreType.DMA((size,)),
             pltpu.SemaphoreType.DMA((len(tiles),)),
-        ],
+        ]
+        + [pltpu.VMEM((depth, w), wq.dtype) for _, w in tiles],
         compiler_params=pltpu.CompilerParams(vmem_limit_bytes=PROJECT_LIMIT),
         cost_estimate=pl.CostEstimate(
             flops=2 * size * tokens * depth * width,

time: 93.2 us -> 93 us (level)
  no operation moved by 1% of the time
where the time goes in v4:
time: 93 us; the launch traced here: 92.5 us
  waiting for transfers between devices  46.9 us (50%)
  starting transfers between devices  26.2 us (28%)
  Pallas kernels  18.2 us (20%)
    ppermute x4, waiting for transfers between devices, hop(): lax.ppermute(x, axis, [(2 * c + p, 2 * (c + step) + p) for c in range(fir...  15.5 us
    pallas_call x1, Pallas kernels, project(): pl.pallas_call(functools.partial(project_kernel, tiles=tiles, counts=coun...  10.2 us
    ppermute x3, waiting for transfers between devices, swap(): lax.ppermute(x, axis, [(2 * c + p, 2 * c + 1 - p) for c in range(first, l...  10.2 us
    ppermute x4, starting transfers between devices, hop(): lax.ppermute(x, axis, [(2 * c + p, 2 * (c + step) + p) for c in range(fir...  8.2 us
    ppermute x1, waiting for transfers between devices, gather_blocks(): lax.ppermute(both, axis, [(2 * a + p, 2 * b + p) for a, b in ends for p i...  6.97 us
    pallas_call x1, Pallas kernels, attend(): pl.pallas_call(kernel, out_shape=jax.ShapeDtypeStruct((seqs, STEPS, QUERY...  5.89 us
    all_to_all x1, waiting for transfers between devices, per_device(): lax.all_to_all(joined, 'tensor', split_axis=0, concat_axis=0, tiled=True)  5.73 us
    ppermute x1, waiting for transfers between devices, gather_blocks(): lax.ppermute(both, axis, [(2 * c + p, 2 * c + 1 - p) for c in (0, 1, line...  5.62 us
  transfers between devices with their start and end apart: 12, of which 9 were waited for; matrix products, arithmetic and copies ran while one was open for 0% of the time, Pallas kernels for 13%

profile of v4, /device:TPU:0, one launch (start us, length us, event | category | flops | bytes accessed | tf_op | source)
XLA Modules:
  0.0 92.5 jit_solution(6061498003632103659)
XLA Ops:
  0.0 5.0 %collective-permute-start.1 = (bf16[8,2,8192]{2,1,0:T(2,128)(2,1)}, bf16[8,2,8192]{2,1,0:T(2,128)(2,1)S(1)}, u32[]{:S(2)}, u32[]{:S(2)}) collective-permute-start(bf16[8,2,8192]{2,1,0:T(2,128)(2,1)} %refs_0_.1), channel_id=1, source_target_pairs={{0,4},{2,6},{4,8},{6,10},{8,12},{10,14},{1,5},{3,7},{5,9},{7,11},{... | collective-permute-start | bytes 786440 | tf_op jit(solution)/shard_map/ppermute | solution.py:241
  5.0 1.3 %collective-permute-start.3 = (bf16[8,2,8192]{2,1,0:T(2,128)(2,1)}, bf16[8,2,8192]{2,1,0:T(2,128)(2,1)S(1)}, u32[]{:S(2)}, u32[]{:S(2)}) collective-permute-start(bf16[8,2,8192]{2,1,0:T(2,128)(2,1)} %refs_0_.1), channel_id=1, source_target_pairs={{4,0},{6,2},{8,4},{10,6},{12,8},{14,10},{5,1},{7,3},{9,5},{11,7},{... | collective-permute-start | bytes 786440 | tf_op jit(solution)/shard_map/ppermute | solution.py:241
  6.3 4.5 %collective-permute-done.1.refs_2_ = bf16[8,2,8192]{2,1,0:T(2,128)(2,1)S(1)} collective-permute-done((bf16[8,2,8192]{2,1,0:T(2,128)(2,1)}, bf16[8,2,8192]{2,1,0:T(2,128)(2,1)S(1)}, u32[]{:S(2)}, u32[]{:S(2)}) %collective-permute-start.1) | collective-permute-done | bytes 262176 | tf_op jit(solution)/shard_map/ppermute | solution.py:241
  10.8 0.7 collective-permute-start.2
  11.5 3.4 %collective-permute-done.3.refs_11_ = bf16[8,2,8192]{2,1,0:T(2,128)(2,1)S(1)} collective-permute-done((bf16[8,2,8192]{2,1,0:T(2,128)(2,1)}, bf16[8,2,8192]{2,1,0:T(2,128)(2,1)S(1)}, u32[]{:S(2)}, u32[]{:S(2)}) %collective-permute-start.3) | collective-permute-done | bytes 262176 | tf_op jit(solution)/shard_map/ppermute | solution.py:241
  14.8 1.3 %collective-permute-start.4 = (bf16[8,2,8192]{2,1,0:T(2,128)(2,1)S(1)}, bf16[8,2,8192]{2,1,0:T(2,128)(2,1)S(1)}, u32[]{:S(2)}, u32[]{:S(2)}) collective-permute-start(bf16[8,2,8192]{2,1,0:T(2,128)(2,1)S(1)} %collective-permute-done.3.refs_11_), channel_id=1, source_target_pairs={{4,0},{6,2},{8,4},{10,6},{5,1},{7,3},{9,5},{11,7},{20,16},{22,18},... | collective-permute-start | bytes 786440 | tf_op jit(solution)/shard_map/ppermute | solution.py:241
  16.1 0.0 collective-permute-done.2.refs_6_
  16.2 7.6 %collective-permute-done.4.refs_7_ = bf16[8,2,8192]{2,1,0:T(2,128)(2,1)S(1)} collective-permute-done((bf16[8,2,8192]{2,1,0:T(2,128)(2,1)S(1)}, bf16[8,2,8192]{2,1,0:T(2,128)(2,1)S(1)}, u32[]{:S(2)}, u32[]{:S(2)}) %collective-permute-start.4) | collective-permute-done | bytes 262176 | tf_op jit(solution)/shard_map/ppermute | solution.py:241
  23.8 1.3 %collective-permute-start.5 = (bf16[8,2,8192]{2,1,0:T(2,128)(2,1)S(1)}, bf16[8,2,8192]{2,1,0:T(2,128)(2,1)S(1)}, u32[]{:S(2)}, u32[]{:S(2)}) collective-permute-start(bf16[8,2,8192]{2,1,0:T(2,128)(2,1)S(1)} %bitcast.16), channel_id=1, source_target_pairs={{4,0},{6,2},{8,12},{10,14},{5,1},{7,3},{9,13},{11,15},{20,16},{22,... | collective-permute-start | bytes 786440 | tf_op jit(solution)/shard_map/ppermute | solution.py:260
  25.1 7.0 %collective-permute-done.5.refs_3_.refs_10_ = bf16[8,2,8192]{2,1,0:T(2,128)(2,1)S(1)} collective-permute-done((bf16[8,2,8192]{2,1,0:T(2,128)(2,1)S(1)}, bf16[8,2,8192]{2,1,0:T(2,128)(2,1)S(1)}, u32[]{:S(2)}, u32[]{:S(2)}) %collective-permute-start.5) | collective-permute-done | bytes 262176 | tf_op jit(solution)/shard_map/ppermute | solution.py:260
  32.1 3.5 %all-to-all-start = ((bf16[8,128,256]{2,1,0:T(8,128)(2,1)}), bf16[8,128,256]{2,1,0:T(8,128)(2,1)S(1)}, u32[]{:S(2)}, u32[]{:S(2)}) async-start(bf16[8,128,256]{2,1,0:T(8,128)(2,1)} %param.15), calls=%async_computation | async-start | bytes 1048576 | tf_op jit(solution)/shard_map/all_to_all | solution.py:369
  35.6 1.9 %collective-permute-start = (bf16[8,2,8192]{2,1,0:T(2,128)(2,1)}, bf16[8,2,8192]{2,1,0:T(2,128)(2,1)S(1)}, u32[]{:S(2)}, u32[]{:S(2)}) collective-permute-start(bf16[8,2,8192]{2,1,0:T(2,128)(2,1)} %refs_0_.1), channel_id=1, source_target_pairs={{0,2},{2,0},{4,6},{6,4},{8,10},{10,8},{12,14},{14,12},{1,3},{3,1},... | collective-permute-start | bytes 786440 | tf_op jit(solution)/shard_map/ppermute | solution.py:246
  37.5 0.7 collective-permute-start.6
  38.2 2.1 %collective-permute-start.9 = (bf16[8,2,8192]{2,1,0:T(2,128)(2,1)S(1)}, bf16[8,2,8192]{2,1,0:T(2,128)(2,1)S(1)}, u32[]{:S(2)}, u32[]{:S(2)}) collective-permute-start(bf16[8,2,8192]{2,1,0:T(2,128)(2,1)S(1)} %collective-permute-done.3.refs_11_), channel_id=1, source_target_pairs={{0,2},{2,0},{4,6},{6,4},{8,10},{10,8},{1,3},{3,1},{5,7},{7,5},{9,1... | collective-permute-start | bytes 786440 | tf_op jit(solution)/shard_map/ppermute | solution.py:246
  40.3 1.9 %collective-permute-start.8 = (bf16[8,2,8192]{2,1,0:T(2,128)(2,1)S(1)}, bf16[8,2,8192]{2,1,0:T(2,128)(2,1)S(1)}, u32[]{:S(2)}, u32[]{:S(2)}) collective-permute-start(bf16[8,2,8192]{2,1,0:T(2,128)(2,1)S(1)} %bitcast.17), channel_id=1, source_target_pairs={{0,2},{2,0},{4,6},{6,4},{8,10},{10,8},{12,14},{14,12},{1,3},{3,1},... | collective-permute-start | bytes 786440 | tf_op jit(solution)/shard_map/ppermute | solution.py:261
  42.2 2.1 %collective-permute-start.7 = (bf16[8,2,8192]{2,1,0:T(2,128)(2,1)S(1)}, bf16[8,2,8192]{2,1,0:T(2,128)(2,1)S(1)}, u32[]{:S(2)}, u32[]{:S(2)}) collective-permute-start(bf16[8,2,8192]{2,1,0:T(2,128)(2,1)S(1)} %collective-permute-done.5.refs_3_.refs_10_), channel_id=1, source_target_pairs={{0,2},{2,0},{12,14},{14,12},{1,3},{3,1},{13,15},{15,13},{16,18},{1... | collective-permute-start | bytes 786440 | tf_op jit(solution)/shard_map/ppermute | solution.py:264
  44.3 0.1 stack.54.choice_ref
  44.4 0.1 stack.50.owner_ref
  44.5 0.0 copy-start.1
  44.5 4.5 %collective-permute-done.refs_1_ = bf16[8,2,8192]{2,1,0:T(2,128)(2,1)S(1)} collective-permute-done((bf16[8,2,8192]{2,1,0:T(2,128)(2,1)}, bf16[8,2,8192]{2,1,0:T(2,128)(2,1)S(1)}, u32[]{:S(2)}, u32[]{:S(2)}) %collective-permute-start) | collective-permute-done | bytes 262176 | tf_op jit(solution)/shard_map/ppermute | solution.py:246
  49.1 0.0 collective-permute-done.6.refs_4_
  49.1 5.6 %collective-permute-done.9.refs_13_ = bf16[8,2,8192]{2,1,0:T(2,128)(2,1)S(1)} collective-permute-done((bf16[8,2,8192]{2,1,0:T(2,128)(2,1)S(1)}, bf16[8,2,8192]{2,1,0:T(2,128)(2,1)S(1)}, u32[]{:S(2)}, u32[]{:S(2)}) %collective-permute-start.9) | collective-permute-done | bytes 262176 | tf_op jit(solution)/shard_map/ppermute | solution.py:246
  54.7 5.6 %collective-permute-done.8.refs_8_.refs_9_ = bf16[8,2,8192]{2,1,0:T(2,128)(2,1)S(1)} collective-permute-done((bf16[8,2,8192]{2,1,0:T(2,128)(2,1)S(1)}, bf16[8,2,8192]{2,1,0:T(2,128)(2,1)S(1)}, u32[]{:S(2)}, u32[]{:S(2)}) %collective-permute-start.8) | collective-permute-done | bytes 262176 | tf_op jit(solution)/shard_map/ppermute | solution.py:261
  60.3 2.9 %collective-permute-done.7.refs_5_.refs_12_ = bf16[8,2,8192]{2,1,0:T(2,128)(2,1)S(1)} collective-permute-done((bf16[8,2,8192]{2,1,0:T(2,128)(2,1)S(1)}, bf16[8,2,8192]{2,1,0:T(2,128)(2,1)S(1)}, u32[]{:S(2)}, u32[]{:S(2)}) %collective-permute-start.7) | collective-permute-done | bytes 262176 | tf_op jit(solution)/shard_map/ppermute | solution.py:264
  63.2 10.2 %project.1.token_ref = bf16[8,16,1280]{2,1,0:T(8,128)(2,1)} custom-call(s32[8]{0:T(128)S(1)} %stack.50.owner_ref, s32[8]{0:T(128)S(1)} %stack.54.choice_ref, bf16[8,2,8192]{2,1,0:T(2,128)(2,1)} %refs_0_.1, bf16[8,2,8192]{2,1,0:T(2,128)(2,1)S(1)} %collective-permute-done.refs_1_, bf16[8,2,8192]{2,1,0:T(2,128)(2,1)S(1)} %collective-permute-done.1.refs_2_, ...), custom_call_target="tpu_custom_call" | custom-call | flops 2684354560 | bytes 23068672 | tf_op jit(solution)/shard_map/project/pallas_call | solution.py:344
  73.4 0.0 copy-start
  73.4 0.0 all-to-all-done.prompt_ref
  73.4 4.6 %all-to-all-start.1 = ((bf16[8,16,1280]{2,1,0:T(8,128)(2,1)}), bf16[8,16,1280]{2,1,0:T(8,128)(2,1)S(1)}, u32[]{:S(2)}, u32[]{:S(2)}) async-start(bf16[8,16,1280]{2,1,0:T(8,128)(2,1)} %project.1.token_ref), calls=%async_computation.1 | async-start | bytes 655360 | tf_op jit(solution)/shard_map/all_to_all | solution.py:372
  78.0 0.0 copy-done.1
  78.0 0.1 copy.10
  78.1 0.1 reshape.4.table_ref
  78.8 2.1 %early.1.early_ref = bf16[2,256,2048]{2,1,0:T(8,128)(2,1)S(1)} custom-call(s32[16]{0:T(128)S(1)} %reshape.4.table_ref, bf16[8,16,1280]{2,1,0:T(8,128)(2,1)} %project.1.token_ref, bf16[16,128,2048]{2,1,0:T(8,128)(2,1)} %pool_ref.3), custom_call_target="tpu_custom_call" | custom-call | bytes 4194304 | tf_op jit(solution)/shard_map/early/pallas_call | solution.py:223
  80.9 5.7 %all-to-all-done.1.q_ref.kv_ref = bf16[8,16,1280]{2,1,0:T(8,128)(2,1)S(1)} async-done(((bf16[8,16,1280]{2,1,0:T(8,128)(2,1)}), bf16[8,16,1280]{2,1,0:T(8,128)(2,1)S(1)}, u32[]{:S(2)}, u32[]{:S(2)}) %all-to-all-start.1) | async-done | bytes 327712 | tf_op jit(solution)/shard_map/all_to_all | solution.py:372
  86.6 0.0 copy-done
  86.6 5.9 %attend.1 = bf16[8,2,8192]{2,1,0:T(2,128)(2,1)} custom-call(s32[16]{0:T(128)S(1)} %reshape.4.table_ref, s32[8]{0:T(128)S(1)} %copy-done, s32[1]{0:T(128)S(6)} %copy.11.slot_ref, bf16[8,16,1280]{2,1,0:T(8,128)(2,1)S(1)} %all-to-all-done.1.q_ref.kv_ref, bf16[8,16,1280]{2,1,0:T(8,128)(2,1)S(1)} %all-to-all-done.1.q_ref.kv_ref, ...), custom_call_target="tpu_custom_call" | custom-call | tf_op jit(solution)/shard_map/attend/pallas_call | solution.py:185
  (2 shorter events, 0.0 us)
Async XLA Ops:
  0.0 10.8 %collective-permute-start.1 = (bf16[8,2,8192]{2,1,0:T(2,128)(2,1)}, bf16[8,2,8192]{2,1,0:T(2,128)(2,1)S(1)}, u32[]{:S(2)}, u32[]{:S(2)}) collective-permute-start(bf16[8,2,8192]{2,1,0:T(2,128)(2,1)} %refs_0_.1), channel_id=1, source_target_pairs={{0,4},{2,6},{4,8},{6,10},{8,12},{10,14},{1,5},{3,7},{5,9},{7,11},{... | collective-permute-start | bytes 786440 | tf_op jit(solution)/shard_map/ppermute | solution.py:241
  5.0 9.9 %collective-permute-start.3 = (bf16[8,2,8192]{2,1,0:T(2,128)(2,1)}, bf16[8,2,8192]{2,1,0:T(2,128)(2,1)S(1)}, u32[]{:S(2)}, u32[]{:S(2)}) collective-permute-start(bf16[8,2,8192]{2,1,0:T(2,128)(2,1)} %refs_0_.1), channel_id=1, source_target_pairs={{4,0},{6,2},{8,4},{10,6},{12,8},{14,10},{5,1},{7,3},{9,5},{11,7},{... | collective-permute-start | bytes 786440 | tf_op jit(solution)/shard_map/ppermute | solution.py:241
  10.8 5.3 %collective-permute-start.2 = (bf16[8,2,8192]{2,1,0:T(2,128)(2,1)S(1)}, bf16[8,2,8192]{2,1,0:T(2,128)(2,1)S(1)}, u32[]{:S(2)}, u32[]{:S(2)}) collective-permute-start(bf16[8,2,8192]{2,1,0:T(2,128)(2,1)S(1)} %collective-permute-done.1.refs_2_), channel_id=1, source_target_pairs={{4,8},{6,10},{8,12},{10,14},{5,9},{7,11},{9,13},{11,15},{20,24},{2... | collective-permute-start | bytes 786440 | tf_op jit(solution)/shard_map/ppermute | solution.py:241
  14.8 8.9 %collective-permute-start.4 = (bf16[8,2,8192]{2,1,0:T(2,128)(2,1)S(1)}, bf16[8,2,8192]{2,1,0:T(2,128)(2,1)S(1)}, u32[]{:S(2)}, u32[]{:S(2)}) collective-permute-start(bf16[8,2,8192]{2,1,0:T(2,128)(2,1)S(1)} %collective-permute-done.3.refs_11_), channel_id=1, source_target_pairs={{4,0},{6,2},{8,4},{10,6},{5,1},{7,3},{9,5},{11,7},{20,16},{22,18},... | collective-permute-start | bytes 786440 | tf_op jit(solution)/shard_map/ppermute | solution.py:241
  23.8 8.3 %collective-permute-start.5 = (bf16[8,2,8192]{2,1,0:T(2,128)(2,1)S(1)}, bf16[8,2,8192]{2,1,0:T(2,128)(2,1)S(1)}, u32[]{:S(2)}, u32[]{:S(2)}) collective-permute-start(bf16[8,2,8192]{2,1,0:T(2,128)(2,1)S(1)} %bitcast.16), channel_id=1, source_target_pairs={{4,0},{6,2},{8,12},{10,14},{5,1},{7,3},{9,13},{11,15},{20,16},{22,... | collective-permute-start | bytes 786440 | tf_op jit(solution)/shard_map/ppermute | solution.py:260
  32.1 41.3 %all-to-all-start = ((bf16[8,128,256]{2,1,0:T(8,128)(2,1)}), bf16[8,128,256]{2,1,0:T(8,128)(2,1)S(1)}, u32[]{:S(2)}, u32[]{:S(2)}) async-start(bf16[8,128,256]{2,1,0:T(8,128)(2,1)} %param.15), calls=%async_computation | async-start | bytes 1048576 | tf_op jit(solution)/shard_map/all_to_all | solution.py:369
  35.6 13.5 %collective-permute-start = (bf16[8,2,8192]{2,1,0:T(2,128)(2,1)}, bf16[8,2,8192]{2,1,0:T(2,128)(2,1)S(1)}, u32[]{:S(2)}, u32[]{:S(2)}) collective-permute-start(bf16[8,2,8192]{2,1,0:T(2,128)(2,1)} %refs_0_.1), channel_id=1, source_target_pairs={{0,2},{2,0},{4,6},{6,4},{8,10},{10,8},{12,14},{14,12},{1,3},{3,1},... | collective-permute-start | bytes 786440 | tf_op jit(solution)/shard_map/ppermute | solution.py:246
  37.5 11.6 %collective-permute-start.6 = (bf16[8,2,8192]{2,1,0:T(2,128)(2,1)S(1)}, bf16[8,2,8192]{2,1,0:T(2,128)(2,1)S(1)}, u32[]{:S(2)}, u32[]{:S(2)}) collective-permute-start(bf16[8,2,8192]{2,1,0:T(2,128)(2,1)S(1)} %collective-permute-done.1.refs_2_), channel_id=1, source_target_pairs={{4,6},{6,4},{8,10},{10,8},{12,14},{14,12},{5,7},{7,5},{9,11},{11,9... | collective-permute-start | bytes 786440 | tf_op jit(solution)/shard_map/ppermute | solution.py:246
  38.2 16.5 %collective-permute-start.9 = (bf16[8,2,8192]{2,1,0:T(2,128)(2,1)S(1)}, bf16[8,2,8192]{2,1,0:T(2,128)(2,1)S(1)}, u32[]{:S(2)}, u32[]{:S(2)}) collective-permute-start(bf16[8,2,8192]{2,1,0:T(2,128)(2,1)S(1)} %collective-permute-done.3.refs_11_), channel_id=1, source_target_pairs={{0,2},{2,0},{4,6},{6,4},{8,10},{10,8},{1,3},{3,1},{5,7},{7,5},{9,1... | collective-permute-start | bytes 786440 | tf_op jit(solution)/shard_map/ppermute | solution.py:246
  40.3 20.0 %collective-permute-start.8 = (bf16[8,2,8192]{2,1,0:T(2,128)(2,1)S(1)}, bf16[8,2,8192]{2,1,0:T(2,128)(2,1)S(1)}, u32[]{:S(2)}, u32[]{:S(2)}) collective-permute-start(bf16[8,2,8192]{2,1,0:T(2,128)(2,1)S(1)} %bitcast.17), channel_id=1, source_target_pairs={{0,2},{2,0},{4,6},{6,4},{8,10},{10,8},{12,14},{14,12},{1,3},{3,1},... | collective-permute-start | bytes 786440 | tf_op jit(solution)/shard_map/ppermute | solution.py:261
  42.2 21.0 %collective-permute-start.7 = (bf16[8,2,8192]{2,1,0:T(2,128)(2,1)S(1)}, bf16[8,2,8192]{2,1,0:T(2,128)(2,1)S(1)}, u32[]{:S(2)}, u32[]{:S(2)}) collective-permute-start(bf16[8,2,8192]{2,1,0:T(2,128)(2,1)S(1)} %collective-permute-done.5.refs_3_.refs_10_), channel_id=1, source_target_pairs={{0,2},{2,0},{12,14},{14,12},{1,3},{3,1},{13,15},{15,13},{16,18},{1... | collective-permute-start | bytes 786440 | tf_op jit(solution)/shard_map/ppermute | solution.py:264
  44.5 33.5 %copy-start.1 = (s32[8,2]{0,1:T(2,128)S(1)}, s32[8,2]{0,1:T(2,128)}, u32[]{:S(2)}) copy-start(s32[8,2]{0,1:T(2,128)} %param.12) | copy-start | bytes 196
  73.4 13.3 %copy-start = (s32[8]{0:T(128)S(1)}, s32[8]{0:T(128)}, u32[]{:S(2)}) copy-start(s32[8]{0:T(128)} %lens_ref.1) | copy-start | bytes 100
  73.4 13.3 %all-to-all-start.1 = ((bf16[8,16,1280]{2,1,0:T(8,128)(2,1)}), bf16[8,16,1280]{2,1,0:T(8,128)(2,1)S(1)}, u32[]{:S(2)}, u32[]{:S(2)}) async-start(bf16[8,16,1280]{2,1,0:T(8,128)(2,1)} %project.1.token_ref), calls=%async_computation.1 | async-start | bytes 655360 | tf_op jit(solution)/shard_map/all_to_all | solution.py:372
